TPU v7x, 32 devices: a whole 2x2x4 slice. The times are simulated.
32 devices in a mesh: dp: 16 (over z, y, core), tensor: 2 (over x).
Axes of the slice: x: 2, y: 2, z: 4, core: 2. Of those that a mesh axis runs over, the one named last changes fastest.
Arguments:
- block_input: bfloat16 [32768, 1024], P(('dp', 'tensor')), may hold values from -6 to 6
- mixer_gain: float32 [1024], replicated, may hold values from 0.25 to 1.75
- in_weight: bfloat16 [1024, 3, 1024], P(None, None, 'tensor'), may hold values from -0.1875 to 0.1875
- conv_kernel: bfloat16 [3, 1024], P(None, 'tensor'), may hold values from -3.5 to 3.5
- out_weight: bfloat16 [1024, 1024], P('tensor'), may hold values from -0.1875 to 0.1875
- ffn_gain: float32 [1024], replicated, may hold values from 0.25 to 1.75
- gate_weight: bfloat16 [1024, 4608], P(None, 'tensor'), may hold values from -0.1875 to 0.1875
- up_weight: bfloat16 [1024, 4608], P(None, 'tensor'), may hold values from -0.1875 to 0.1875
- down_weight: bfloat16 [4608, 1024], P('tensor'), may hold values from -0.09375 to 0.09375
- output_grad: bfloat16 [32768, 1024], P(('dp', 'tensor')), may hold values from -6 to 6
- lengths: int32 [32], P('dp'), may hold values from 256 to 1024, as said below
Outputs:
- block_output: bfloat16 [32768, 1024], P(('dp', 'tensor'))
- input_grad: bfloat16 [32768, 1024], P(('dp', 'tensor'))
- mixer_gain_grad: float32 [1024], replicated
- in_weight_grad: float32 [1024, 3, 1024], P(None, None, 'tensor')
- conv_kernel_grad: float32 [3, 1024], P(None, 'tensor')
- out_weight_grad: float32 [1024, 1024], P('tensor')
- ffn_gain_grad: float32 [1024], replicated
- gate_weight_grad: float32 [1024, 4608], P(None, 'tensor')
- up_weight_grad: float32 [1024, 4608], P(None, 'tensor')
- down_weight_grad: float32 [4608, 1024], P('tensor')
Inputs may be any that keep to these rules, and one draw needn't show every extreme that they name: `lengths`: each slot holds one sequence at positions 0 to its length - 1; some slot has length 1024 and some 1024 // 4.
All inputs are finite; a program needn't handle non-finite values.
Results may differ from a plain program's by a relative error of at most 0.022.
Values may be sent and summed in bfloat16 or wider, within the bound.
A program may use at most 256 MiB of HBM per device.

v0:
```python
import jax
import jax.numpy as jnp
from jax import lax
from jax.sharding import PartitionSpec as P

KERNEL = 3


eps = 1e-05


def rms_forward(values, gain_values):
    inverse = lax.rsqrt(jnp.mean(values * values, axis=-1, keepdims=True) + eps)
    return (values * inverse * gain_values, inverse)


def rms_backward(values, inverse, gain_values, upstream):
    weighted = upstream * gain_values
    gain_part = jnp.sum(upstream * values * inverse, axis=0)
    through = inverse * weighted - values * inverse**3 * jnp.mean(
        weighted * values, axis=-1, keepdims=True
    )
    return (through, gain_part)


def local(
    block_input,
    mixer_gain,
    in_weight,
    conv_kernel,
    out_weight,
    ffn_gain,
    gate_weight,
    up_weight,
    down_weight,
    output_grad,
    lengths,
):
    local_rows = block_input.shape[0]
    model_width = block_input.shape[1]
    channels = in_weight.shape[2]
    slot_count = lengths.shape[0]
    source = block_input.astype(jnp.float32)
    normed_one, inverse_one = rms_forward(source, mixer_gain)
    gathered_one = lax.all_gather(normed_one.astype(jnp.bfloat16), "tensor", axis=0, tiled=True)
    group_rows = gathered_one.shape[0]
    slot_length = group_rows // slot_count
    in_flat = in_weight.reshape(model_width, 3 * channels)
    projected = jnp.dot(gathered_one, in_flat, preferred_element_type=jnp.float32).reshape(
        group_rows, 3, channels
    )
    b_part = projected[:, 0]
    c_part = projected[:, 1]
    x_part = projected[:, 2]
    mixed = (b_part * x_part).reshape(slot_count, slot_length, channels)
    kernel_values = conv_kernel.astype(jnp.float32)
    padded = jnp.pad(mixed, ((0, 0), (KERNEL - 1, 0), (0, 0)))
    convolved = jnp.zeros_like(mixed)
    for offset in range(KERNEL):
        convolved = convolved + kernel_values[offset] * padded[:, offset : offset + slot_length]
    convolved = convolved.reshape(group_rows, channels)
    gated = (c_part * convolved).astype(jnp.bfloat16)
    hidden = source + lax.psum_scatter(
        jnp.dot(gated, out_weight, preferred_element_type=jnp.float32).astype(jnp.bfloat16),
        "tensor",
        scatter_dimension=0,
        tiled=True,
    ).astype(jnp.float32)
    normed_two, inverse_two = rms_forward(hidden, ffn_gain)
    gathered_two = lax.all_gather(normed_two.astype(jnp.bfloat16), "tensor", axis=0, tiled=True)
    gate_value = jnp.dot(gathered_two, gate_weight, preferred_element_type=jnp.float32)
    up_value = jnp.dot(gathered_two, up_weight, preferred_element_type=jnp.float32)
    sigmoid_gate = jax.nn.sigmoid(gate_value)
    silu_value = gate_value * sigmoid_gate
    inner_low = (silu_value * up_value).astype(jnp.bfloat16)
    block_output = (
        hidden
        + lax.psum_scatter(
            jnp.dot(inner_low, down_weight, preferred_element_type=jnp.float32).astype(
                jnp.bfloat16
            ),
            "tensor",
            scatter_dimension=0,
            tiled=True,
        ).astype(jnp.float32)
    ).astype(jnp.bfloat16)
    row_index = lax.axis_index("tensor") * local_rows + jnp.arange(local_rows, dtype=jnp.int32)
    slot_of = row_index // slot_length
    position = row_index % slot_length
    matched = (slot_of[:, None] == jnp.arange(slot_count, dtype=jnp.int32)[None, :]) & (
        position[:, None] < lengths[None, :]
    )
    token_mask = jnp.any(matched, axis=1).astype(jnp.float32)
    cotangent = output_grad.astype(jnp.float32) * token_mask[:, None]
    grad_rows = lax.all_gather(cotangent.astype(jnp.bfloat16), "tensor", axis=0, tiled=True)
    inner_grad = jnp.einsum("rd,fd->rf", grad_rows, down_weight, preferred_element_type=jnp.float32)
    down_weight_grad = jnp.einsum(
        "rf,rd->fd", inner_low, grad_rows, preferred_element_type=jnp.float32
    )
    gate_grad = (
        inner_grad * up_value * sigmoid_gate * (1.0 + gate_value * (1.0 - sigmoid_gate))
    ).astype(jnp.bfloat16)
    up_grad = (inner_grad * silu_value).astype(jnp.bfloat16)
    gate_weight_grad = jnp.einsum(
        "rd,rf->df", gathered_two, gate_grad, preferred_element_type=jnp.float32
    )
    up_weight_grad = jnp.einsum(
        "rd,rf->df", gathered_two, up_grad, preferred_element_type=jnp.float32
    )
    from_gate = jnp.einsum("rf,df->rd", gate_grad, gate_weight, preferred_element_type=jnp.float32)
    normed_two_grad = lax.psum_scatter(
        (
            from_gate
            + jnp.einsum("rf,df->rd", up_grad, up_weight, preferred_element_type=jnp.float32)
        ).astype(jnp.bfloat16),
        "tensor",
        scatter_dimension=0,
        tiled=True,
    ).astype(jnp.float32)
    through_two, ffn_gain_part = rms_backward(hidden, inverse_two, ffn_gain, normed_two_grad)
    hidden_grad = cotangent + through_two
    hidden_rows = lax.all_gather(hidden_grad.astype(jnp.bfloat16), "tensor", axis=0, tiled=True)
    gated_grad = jnp.einsum(
        "rd,cd->rc", hidden_rows, out_weight, preferred_element_type=jnp.float32
    )
    out_weight_grad = jnp.einsum(
        "rc,rd->cd", gated, hidden_rows, preferred_element_type=jnp.float32
    )
    c_grad = gated_grad * convolved
    conv_grad = (gated_grad * c_part).reshape(slot_count, slot_length, channels)
    padded_after = jnp.pad(conv_grad, ((0, 0), (0, KERNEL - 1), (0, 0)))
    mixed_grad = jnp.zeros_like(conv_grad)
    kernel_rows = []
    for offset in range(KERNEL):
        shift_start = KERNEL - 1 - offset
        mixed_grad = (
            mixed_grad
            + kernel_values[offset] * padded_after[:, shift_start : shift_start + slot_length]
        )
        kernel_rows.append(
            jnp.sum(conv_grad * padded[:, offset : offset + slot_length], axis=(0, 1))
        )
    conv_kernel_grad = jnp.stack(kernel_rows, axis=0)
    mixed_grad = mixed_grad.reshape(group_rows, channels)
    projected_grad = jnp.stack([mixed_grad * x_part, c_grad, mixed_grad * b_part], axis=1).astype(
        jnp.bfloat16
    )
    in_weight_grad = jnp.einsum(
        "rd,rkc->dkc", gathered_one, projected_grad, preferred_element_type=jnp.float32
    )
    normed_one_grad = lax.psum_scatter(
        jnp.einsum(
            "rkc,dkc->rd", projected_grad, in_weight, preferred_element_type=jnp.float32
        ).astype(jnp.bfloat16),
        "tensor",
        scatter_dimension=0,
        tiled=True,
    ).astype(jnp.float32)
    through_one, mixer_gain_part = rms_backward(source, inverse_one, mixer_gain, normed_one_grad)
    input_grad = (hidden_grad + through_one).astype(jnp.bfloat16)
    (
        in_weight_grad,
        conv_kernel_grad,
        out_weight_grad,
        gate_weight_grad,
        up_weight_grad,
        down_weight_grad,
    ) = (
        lax.psum(in_weight_grad.astype(jnp.bfloat16), "dp").astype(jnp.float32),
        lax.psum(conv_kernel_grad.astype(jnp.bfloat16), "dp").astype(jnp.float32),
        lax.psum(out_weight_grad.astype(jnp.bfloat16), "dp").astype(jnp.float32),
        lax.psum(gate_weight_grad.astype(jnp.bfloat16), "dp").astype(jnp.float32),
        lax.psum(up_weight_grad.astype(jnp.bfloat16), "dp").astype(jnp.float32),
        lax.psum(down_weight_grad.astype(jnp.bfloat16), "dp").astype(jnp.float32),
    )
    mixer_gain_grad, ffn_gain_grad = lax.psum((mixer_gain_part, ffn_gain_part), ("dp", "tensor"))
    return (
        block_output,
        input_grad,
        mixer_gain_grad,
        in_weight_grad,
        conv_kernel_grad,
        out_weight_grad,
        ffn_gain_grad,
        gate_weight_grad,
        up_weight_grad,
        down_weight_grad,
    )


def solution(mesh):
    return jax.shard_map(
        local,
        mesh=mesh,
        in_specs=(
            P(("dp", "tensor"), None),
            P(),
            P(None, None, "tensor"),
            P(None, "tensor"),
            P("tensor", None),
            P(),
            P(None, "tensor"),
            P(None, "tensor"),
            P("tensor", None),
            P(("dp", "tensor"), None),
            P("dp"),
        ),
        out_specs=(
            P(("dp", "tensor"), None),
            P(("dp", "tensor"), None),
            P(),
            P(None, None, "tensor"),
            P(None, "tensor"),
            P("tensor", None),
            P(),
            P(None, "tensor"),
            P(None, "tensor"),
            P("tensor", None),
        ),
        check_vma=False,
    )
```

profile of v0, /device:TPU:0, one launch (start us, length us, event | category | flops | bytes accessed | tf_op | source)
XLA Modules:
  0.0 967.9 jit_solution(12564560113143871038)
XLA Ops:
  18.8 54.9 %all-gather.5.cloned.1.call-done = bf16[2048,1024]{1,0:T(8,128)(2,1)} async-done(((bf16[1024,1024]{1,0:T(8,128)(2,1)}), bf16[2048,1024]{1,0:T(8,128)(2,1)}) %all-gather.5.cloned.1.call-update) | async-done | bytes 4194320 | tf_op jit(solution)/shard_map/all_gather | solution.py:45
  73.7 9.5 fusion.26
  96.6 54.4 %reduce-scatter.5.cloned.1.call-done = bf16[1024,1024]{1,0:T(8,128)(2,1)} async-done(((bf16[2048,1024]{1,0:T(8,128)(2,1)}), bf16[1024,1024]{1,0:T(8,128)(2,1)}) %reduce-scatter.5.cloned.1.call-update) | async-done | bytes 2097168 | tf_op jit(solution)/shard_map/reduce_scatter | solution.py:63
  161.2 52.6 %all-gather.7.cloned.1.call-done = bf16[2048,1024]{1,0:T(8,128)(2,1)} async-done(((bf16[1024,1024]{1,0:T(8,128)(2,1)}), bf16[2048,1024]{1,0:T(8,128)(2,1)}) %all-gather.7.cloned.1.call-update) | async-done | bytes 4194320 | tf_op jit(solution)/shard_map/all_gather | solution.py:70
  213.7 16.9 %fusion.46 = f32[2048,2304]{1,0:T(8,128)} fusion(bf16[2048,1024]{1,0:T(8,128)(2,1)} %all-gather.7.cloned.1.call-done, bf16[1024,2304]{1,0:T(8,128)(2,1)} %param.18), kind=kOutput, calls=%fused_computation.96 | convolution fusion | flops 9663676416 | bytes 27787264 | tf_op jit(solution)/shard_map/dot_general | solution.py:72
  230.6 15.3 %fusion.45 = f32[2048,2304]{1,0:T(8,128)} fusion(bf16[2048,1024]{1,0:T(8,128)(2,1)S(1)} %copy-done.37, bf16[1024,2304]{1,0:T(8,128)(2,1)} %param.17), kind=kOutput, calls=%fused_computation.95 | convolution fusion | flops 9663676416 | bytes 27787264 | tf_op jit(solution)/shard_map/dot_general | solution.py:71
  245.9 26.7 %all-gather.9.cloned.1.call-done = bf16[2048,1024]{1,0:T(8,128)(2,1)} async-done(((bf16[1024,1024]{1,0:T(8,128)(2,1)}), bf16[2048,1024]{1,0:T(8,128)(2,1)}) %all-gather.9.cloned.1.call-update) | async-done | bytes 4194320 | tf_op jit(solution)/shard_map/all_gather | solution.py:95
  272.6 35.7 %multiply_convert_fusion = (bf16[2048,2304]{1,0:T(8,128)(2,1)}, bf16[2048,2304]{1,0:T(8,128)(2,1)}, bf16[2048,2304]{1,0:T(8,128)(2,1)}) fusion(f32[2048,2304]{1,0:T(8,128)} %fusion.45, f32[2048,2304]{1,0:T(8,128)} %fusion.46, bf16[2048,1024]{1,0:T(8,128)(2,1)} %all-gather.9.cloned.1.call-done, bf16[2304,1024]{1,0:T(8,128)(2,1)} %param.19), kind=kOutput, calls=%fused_computation | convolution fusion | flops 9734455296 | bytes 74973184 | tf_op jit(solution)/shard_map/rd,fd->rf/dot_general | solution.py:96
  308.3 14.0 %fusion.47 = f32[2048,1024]{1,0:T(8,128)S(1)} fusion(bf16[2048,2304]{1,0:T(8,128)(2,1)} %get-tuple-element.27, bf16[1024,2304]{1,0:T(8,128)(2,1)} %param.17), kind=kOutput, calls=%fused_computation.97 | convolution fusion | flops 9663676416 | bytes 22544384 | tf_op jit(solution)/shard_map/rf,df->rd/dot_general | solution.py:110
  322.3 14.3 %add_convert_fusion = bf16[2048,1024]{1,0:T(8,128)(2,1)} fusion(f32[2048,1024]{1,0:T(8,128)S(1)} %fusion.47, bf16[2048,2304]{1,0:T(8,128)(2,1)S(1)} %copy-done.39, bf16[1024,2304]{1,0:T(8,128)(2,1)} %param.18), kind=kOutput, calls=%fused_computation.12 | convolution fusion | flops 9667870720 | bytes 26738688 | tf_op jit(solution)/shard_map/rf,df->rd/dot_general | solution.py:114
  336.8 15.2 %convolution_convert_fusion.3 = bf16[2048,1024]{1,0:T(8,128)(2,1)} fusion(bf16[2048,2304]{1,0:T(8,128)(2,1)} %get-tuple-element.28, bf16[2304,1024]{1,0:T(8,128)(2,1)} %param.19), kind=kOutput, calls=%fused_computation.66 | convolution fusion | flops 9665773568 | bytes 18350080 | tf_op jit(solution)/shard_map/dot_general | solution.py:79
  352.1 39.1 %reduce-scatter.9.cloned.1.call-done = bf16[1024,1024]{1,0:T(8,128)(2,1)} async-done(((bf16[2048,1024]{1,0:T(8,128)(2,1)}), bf16[1024,1024]{1,0:T(8,128)(2,1)}) %reduce-scatter.9.cloned.1.call-update) | async-done | bytes 2097168 | tf_op jit(solution)/shard_map/reduce_scatter | solution.py:111
  395.1 52.5 %reduce-scatter.7.cloned.1.call-done = bf16[1024,1024]{1,0:T(8,128)(2,1)} async-done(((bf16[2048,1024]{1,0:T(8,128)(2,1)}), bf16[1024,1024]{1,0:T(8,128)(2,1)}) %reduce-scatter.7.cloned.1.call-update) | async-done | bytes 2097168 | tf_op jit(solution)/shard_map/reduce_scatter | solution.py:78
  454.5 56.9 %all-gather.11.cloned.1.call-done = bf16[2048,1024]{1,0:T(8,128)(2,1)} async-done(((bf16[1024,1024]{1,0:T(8,128)(2,1)}), bf16[2048,1024]{1,0:T(8,128)(2,1)}) %all-gather.11.cloned.1.call-update) | async-done | bytes 4194320 | tf_op jit(solution)/shard_map/all_gather | solution.py:122
  511.4 10.5 %multiply_reduce_fusion.1 = (bf16[512]{0:T(512)(128)(2,1)S(1)}, bf16[512]{0:T(512)(128)(2,1)S(1)}, f32[2048,512]{1,0:T(8,128)}, f32[2048,512]{1,0:T(8,128)}) fusion(f32[2,1024,512]{2,1,0:T(8,128)} %bitcast.78, f32[2048,3,512]{2,0,1:T(8,128)} %copy-done.3, bf16[2048,1024]{1,0:T(8,128)(2,1)} %all-gather.11.cloned.1.call-done, bf16[512,1024]{1,0:T(8,128)(2,1)S(1)} %copy-done), kind=kOutput, calls=%fused_computation.54 | convolution fusion | flops 2152725504 | bytes 22022144 | tf_op jit(solution)/shard_map/rd,cd->rc/dot_general | solution.py:123
  527.0 8.4 multiply_add_fusion
  541.5 10.1 %bitcast_convert_fusion = bf16[2048,1024]{1,0:T(8,128)(2,1)} fusion(bf16[1024,3,512]{2,0,1:T(8,128)(2,1)S(1)} %copy-done.10, bf16[2048,1,512]{2,0,1:T(8,128)(2,1)} %get-tuple-element.30, bf16[2048,1,512]{2,0,1:T(8,128)(2,1)} %bitcast.84, bf16[2048,1,512]{2,0,1:T(8,128)(2,1)} %get-tuple-element.29), kind=kOutput, calls=%fused_computation.11 | convolution fusion | flops 6450839552 | bytes 13631488 | tf_op jit(solution)/shard_map/rkc,dkc->rd/dot_general | solution.py:152
  551.7 15.6 %convolution_convert_fusion.2 = bf16[2304,1024]{1,0:T(8,128)(2,1)} fusion(bf16[2048,2304]{1,0:T(8,128)(2,1)} %get-tuple-element.28, bf16[2048,1024]{1,0:T(8,128)(2,1)} %all-gather.9.cloned.1.call-done), kind=kOutput, calls=%fused_computation.16 | convolution fusion | flops 9666035712 | bytes 18350080 | tf_op jit(solution)/shard_map/rf,rd->fd/dot_general | solution.py:97
  567.2 14.1 %convolution_convert_fusion = bf16[1024,2304]{1,0:T(8,128)(2,1)} fusion(bf16[2048,1024]{1,0:T(8,128)(2,1)S(1)} %copy-done.38, bf16[2048,2304]{1,0:T(8,128)(2,1)} %get-tuple-element.26), kind=kOutput, calls=%fused_computation.14 | convolution fusion | flops 9666035712 | bytes 18350080 | tf_op jit(solution)/shard_map/rd,rf->df/dot_general | solution.py:107
  581.4 12.3 %convolution_convert_fusion.1 = bf16[1024,2304]{1,0:T(8,128)(2,1)} fusion(bf16[2048,1024]{1,0:T(8,128)(2,1)S(1)} %copy-done.38, bf16[2048,2304]{1,0:T(8,128)(2,1)S(1)} %bitcast.93), kind=kOutput, calls=%fused_computation.15 | convolution fusion | flops 9666035712 | bytes 18350080 | tf_op jit(solution)/shard_map/rd,rf->df/dot_general | solution.py:104
  598.3 8.5 fusion.31
  612.4 34.8 %psum.58 = bf16[3,512]{1,0:T(4,128)(2,1)S(1)} all-reduce(bf16[3,512]{1,0:T(4,128)(2,1)S(1)} %pad_maximum_fusion.5), channel_id=1, replica_groups=mesh['dp'=16,'tensor'=2] {'dp'}, use_global_device_ids=true, to_apply=%region_15.16 | all-reduce | flops 1536 | bytes 6144 | tf_op jit(solution)/shard_map/psum | solution.py:170
  651.1 38.5 %all-reduce.2 = (f32[1024]{0:T(1024)}, f32[1024]{0:T(1024)}) all-reduce(f32[1024]{0:T(1024)S(1)} %get-tuple-element.14, f32[1024]{0:T(1024)S(1)} %get-tuple-element.12), channel_id=1, replica_groups=mesh['dp'=16,'tensor'=2] {'dp','tensor'}, use_global_device_ids=true, to_apply=%region_10.11 | all-reduce | flops 2048 | bytes 16384 | tf_op jit(solution)/shard_map/psum | solution.py:176
  694.2 245.0 %all-reduce.6.cloned.1.call-done = (bf16[1024,3,512]{2,0,1:T(8,128)(2,1)}, bf16[512,1024]{1,0:T(8,128)(2,1)}, bf16[1024,2304]{1,0:T(8,128)(2,1)}, bf16[1024,2304]{1,0:T(8,128)(2,1)}, bf16[2304,1024]{1,0:T(8,128)(2,1)}) async-done(((bf16[1024,3,512]{2,0,1:T(8,128)(2,1)}, bf16[512,1024]{1,0:T(8,128)(2,1)}, bf16[1024,2304]{1,0:T(8,128)(2,1)}, bf16[1024,2304]{1,0:T(8,128)(2,1)}, bf16[2304,1024]{1,0:T(8,128)(2,1)}), ...) | async-done | bytes 18350096 | tf_op jit(solution)/shard_map/psum | solution.py:169
  (159 shorter events, 97.6 us)
Async XLA Ops:
  7.2 85.0 %copy-start = (bf16[512,1024]{1,0:T(8,128)(2,1)S(1)}, bf16[512,1024]{1,0:T(8,128)(2,1)}, u32[]{:S(2)}) copy-start(bf16[512,1024]{1,0:T(8,128)(2,1)} %param.15) | copy-start | bytes 3145732
  7.2 66.5 %all-gather.5.cloned.1.call-start = ((), (), s32[]{:S(2)}) async-start(), calls=%async_computation.4 | async-start | bytes 6291456 | tf_op jit(solution)/shard_map/all_gather | solution.py:45
  14.1 137.0 %reduce-scatter.5.cloned.1.call-start = ((), (), s32[]{:S(2)}) async-start(), calls=%async_computation.5 | async-start | bytes 6291456 | tf_op jit(solution)/shard_map/reduce_scatter | solution.py:63
  18.8 65.5 %copy-start.26 = (f32[1,512]{1,0:T(1,128)}, f32[1,512]{1,0:T(1,128)S(1)}, u32[]{:S(2)}) copy-start(f32[1,512]{1,0:T(1,128)S(1)} %get-tuple-element.36) | copy-start | bytes 6148
  18.8 65.5 %copy-start.28 = (f32[1,512]{1,0:T(1,128)}, f32[1,512]{1,0:T(1,128)S(1)}, u32[]{:S(2)}) copy-start(f32[1,512]{1,0:T(1,128)S(1)} %get-tuple-element.37) | copy-start | bytes 6148
  18.8 65.5 %copy-start.30 = (f32[1,512]{1,0:T(1,128)}, f32[1,512]{1,0:T(1,128)S(1)}, u32[]{:S(2)}) copy-start(f32[1,512]{1,0:T(1,128)S(1)} %get-tuple-element.38) | copy-start | bytes 6148
  96.5 54.5 %copy-start.1 = (bf16[1024,1024]{1,0:T(8,128)(2,1)S(1)}, bf16[1024,1024]{1,0:T(8,128)(2,1)}, u32[]{:S(2)}) copy-start(bf16[1024,1024]{1,0:T(8,128)(2,1)} %param.11) | copy-start | bytes 6291460
  96.5 58.2 %copy-start.21 = (f32[1024]{0:T(1024)S(1)}, f32[1024]{0:T(1024)}, u32[]{:S(2)}) copy-start(f32[1024]{0:T(1024)} %param.16) | copy-start | bytes 12292
  96.6 117.2 %all-gather.7.cloned.1.call-start = ((), (), s32[]{:S(2)}) async-start(), calls=%async_computation.6 | async-start | bytes 6291456 | tf_op jit(solution)/shard_map/all_gather | solution.py:70
  156.8 115.7 %all-gather.9.cloned.1.call-start = ((), (), s32[]{:S(2)}) async-start(), calls=%async_computation.8 | async-start | bytes 6291456 | tf_op jit(solution)/shard_map/all_gather | solution.py:95
  161.1 230.1 %reduce-scatter.9.cloned.1.call-start = ((), (), s32[]{:S(2)}) async-start(), calls=%async_computation.9 | async-start | bytes 6291456 | tf_op jit(solution)/shard_map/reduce_scatter | solution.py:111
  336.7 110.9 %reduce-scatter.7.cloned.1.call-start = ((), (), s32[]{:S(2)}) async-start(), calls=%async_computation.7 | async-start | bytes 6291456 | tf_op jit(solution)/shard_map/reduce_scatter | solution.py:78
  351.9 39.2 %copy-start.2 = (bf16[1024,1024]{1,0:T(8,128)(2,1)S(1)}, bf16[1024,1024]{1,0:T(8,128)(2,1)}, u32[]{:S(2)}) copy-start(bf16[1024,1024]{1,0:T(8,128)(2,1)} %param.11) | copy-start | bytes 6291460
  351.9 39.2 %copy-start.20 = (f32[1024]{0:T(1024)S(1)}, f32[1024]{0:T(1024)}, u32[]{:S(2)}) copy-start(f32[1024]{0:T(1024)} %copy-done.19) | copy-start | bytes 12292
  352.0 39.2 %copy-start.22 = (f32[1024]{0:T(1024)S(1)}, f32[1024]{0:T(1024)}, u32[]{:S(2)}) copy-start(f32[1024]{0:T(1024)} %param.16) | copy-start | bytes 12292
  352.0 95.7 %copy-start.25 = (f32[1024]{0:T(1024)S(1)}, f32[1024]{0:T(1024)}, u32[]{:S(2)}) copy-start(f32[1024]{0:T(1024)} %copy-done.24) | copy-start | bytes 12292
  352.0 95.7 %copy-start.33 = (f32[1024]{0:T(1024)S(1)}, f32[1024]{0:T(1024)}, u32[]{:S(2)}) copy-start(f32[1024]{0:T(1024)} %get-tuple-element.34) | copy-start | bytes 12292
  352.0 159.3 %all-gather.11.cloned.1.call-start = ((), (), s32[]{:S(2)}) async-start(), calls=%async_computation.10 | async-start | bytes 6291456 | tf_op jit(solution)/shard_map/all_gather | solution.py:122
  454.4 193.4 %reduce-scatter.11.cloned.1.call-start = ((), (), s32[]{:S(2)}) async-start(), calls=%async_computation.11 | async-start | bytes 6291456 | tf_op jit(solution)/shard_map/reduce_scatter | solution.py:151
  551.6 387.6 %all-reduce.6.cloned.1.call-start = ((), (), s32[]{:S(2)}) async-start(), calls=%async_computation.12 | async-start | bytes 36700160 | tf_op jit(solution)/shard_map/psum | solution.py:169
  551.6 29.7 %slice-start.7 = ((s8[9437184]{0:T(1024)(128)(4,1)}), s8[4194304]{0:T(1024)(128)(4,1)S(1)}, s32[]{:S(2)}) async-start(s8[9437184]{0:T(1024)(128)(4,1)} %bitcast.92), calls=%async_computation.20 | async-start | bytes 8388608
  606.8 41.0 %copy-start.18 = (f32[1024]{0:T(1024)S(1)}, f32[1024]{0:T(1024)}, u32[]{:S(2)}) copy-start(f32[1024]{0:T(1024)} %copy-done.17) | copy-start | bytes 12292
  606.8 41.0 %copy-start.23 = (f32[1024]{0:T(1024)S(1)}, f32[1024]{0:T(1024)}, u32[]{:S(2)}) copy-start(f32[1024]{0:T(1024)} %param.12) | copy-start | bytes 12292
  612.4 77.3 %copy-start.32 = (f32[1024]{0:T(1024)S(1)}, f32[1024]{0:T(1024)}, u32[]{:S(2)}) copy-start(f32[1024]{0:T(1024)} %get-tuple-element.32) | copy-start | bytes 12292
  (35 other events, 284.7 us)
Sparse Core Ops, SparseCore 0:
  14.2 59.4 all-gather.4
  96.7 54.2 reduce-scatter.4
  156.9 56.7 all-gather.6
  215.8 56.7 all-gather.8
  336.8 54.3 reduce-scatter.8
  393.3 54.2 reduce-scatter.6
  454.6 56.7 all-gather.10
  551.7 54.3 reduce-scatter.10
  612.3 326.8 all-reduce.5
where the time goes:
time: 977 us; the launch traced here: 968 us
  waiting for transfers between devices  582 us (60%)
  matrix products  200 us (20%)
  other arithmetic  84.3 us (9%)
  blocking collectives  73.3 us (8%)
  between operations  14.6 us (1%)
  local copies, waits for them, and re-layouts  13.3 us (1%)
    psum x1, waiting for transfers between devices, local(): lax.psum(in_weight_grad.astype(jnp.bfloat16), 'dp').astype(jnp.float32)  245 us
    all_gather x1, waiting for transfers between devices, local(): lax.all_gather(hidden_grad.astype(jnp.bfloat16), 'tensor', axis=0, tiled=...  56.9 us
    all_gather x1, waiting for transfers between devices, local(): lax.all_gather(normed_one.astype(jnp.bfloat16), 'tensor', axis=0, tiled=T...  54.9 us
    reduce_scatter x1, waiting for transfers between devices, local(): lax.psum_scatter(jnp.dot(gated, out_weight, preferred_element_type=jnp.fl...  54.4 us
    all_gather x1, waiting for transfers between devices, local(): lax.all_gather(normed_two.astype(jnp.bfloat16), 'tensor', axis=0, tiled=T...  52.6 us
    reduce_scatter x1, waiting for transfers between devices, local(): lax.psum_scatter(jnp.dot(inner_low, down_weight, preferred_element_type=j...  52.5 us
    reduce_scatter x1, waiting for transfers between devices, local(): lax.psum_scatter((from_gate + jnp.einsum('rf,df->rd', up_grad, up_weight,...  39.1 us
    psum x1, blocking collectives, local(): lax.psum((mixer_gain_part, ffn_gain_part), ('dp', 'tensor'))  38.5 us
  transfers between devices with their start and end apart: 9, of which 8 were waited for; matrix products, arithmetic and copies ran while one was open for 13% of the time, Pallas kernels for 0%

commit v1 on v0

--- a/solution.py
+++ b/solution.py
@@ -1,6 +1,10 @@
+import functools
+
 import jax
 import jax.numpy as jnp
 from jax import lax
+from jax.experimental import pallas as pl
+from jax.experimental.pallas import tpu as pltpu
 from jax.sharding import PartitionSpec as P
 
 KERNEL = 3
@@ -188,9 +192,259 @@
     )
 
 
+NN = (((1,), (0,)), ((), ()))
+NT = (((1,), (1,)), ((), ()))
+TN = (((0,), (0,)), ((), ()))
+F32 = jnp.float32
+BF16 = jnp.bfloat16
+
+
+def dot(a, b, dims=NN):
+    return lax.dot_general(a, b, dims, preferred_element_type=F32)
+
+
+def ffn_kernel(n2, cot, wg, wu, wd, inner, gg, ug, out, n2g, acc1, acc2, *, rows):
+    step = pl.program_id(0)
+
+    @pl.when(step == 0)
+    def _():
+        acc1[...] = jnp.zeros_like(acc1)
+        acc2[...] = jnp.zeros_like(acc2)
+
+    def front(r):
+        s = pl.ds(r * rows, rows)
+        a, c = n2[s, :], cot[s, :]
+        return dot(a, wg[...]), dot(a, wu[...]), dot(c, wd[...], NT)
+
+    count = n2.shape[0] // rows
+    held = front(0)
+    for r in range(count):
+        following = front(r + 1) if r + 1 < count else None
+        s = pl.ds(r * rows, rows)
+        g, u, ig = held
+        sig = jax.nn.sigmoid(g)
+        silu = g * sig
+        low = (silu * u).astype(BF16)
+        gg_low = (ig * u * (sig + silu * (1.0 - sig))).astype(BF16)
+        ug_low = (ig * silu).astype(BF16)
+        inner[s, :] = low
+        gg[s, :] = gg_low
+        ug[s, :] = ug_low
+        acc1[s, :] += dot(low, wd[...])
+        acc2[s, :] += dot(gg_low, wg[...], NT) + dot(ug_low, wu[...], NT)
+        held = following
+
+    @pl.when(step == pl.num_programs(0) - 1)
+    def _():
+        out[...] = acc1[...].astype(out.dtype)
+        n2g[...] = acc2[...].astype(n2g.dtype)
+
+
+def ffn(n2, cot, wg, wu, wd, name):
+    rows, width = n2.shape
+    hidden = wg.shape[1]
+    tile = 256
+    full = pl.BlockSpec((rows, width), lambda h: (0, 0), pipeline_mode=pl.Buffered(1))
+
+    def col(n):
+        return pl.BlockSpec((n, tile), lambda h: (0, h))
+
+    return pl.pallas_call(
+        functools.partial(ffn_kernel, rows=256),
+        grid=(hidden // tile,),
+        in_specs=[full, full, col(width), col(width), pl.BlockSpec((tile, width), lambda h: (h, 0))],
+        out_specs=[col(rows), col(rows), col(rows), full, full],
+        out_shape=[jax.ShapeDtypeStruct((rows, hidden), BF16)] * 3
+        + [jax.ShapeDtypeStruct((rows, width), BF16)] * 2,
+        scratch_shapes=[pltpu.VMEM((rows, width), F32)] * 2,
+        name=name,
+        cost_estimate=pl.CostEstimate(
+            flops=12 * rows * width * hidden,
+            bytes_accessed=6 * hidden * width + 6 * rows * hidden + 8 * rows * width,
+            transcendentals=rows * hidden,
+        ),
+        compiler_params=pltpu.CompilerParams(vmem_limit_bytes=48 * 2**20),
+    )(n2, cot, wg, wu, wd)
+
+
+def shift_down(values, amount):
+    return jnp.pad(values, ((amount, 0), (0, 0)))[: values.shape[0]]
+
+
+def shift_up(values, amount):
+    return jnp.pad(values, ((0, amount), (0, 0)))[amount:]
+
+
+def mixer_forward(normed, in_half, kernel_half):
+    channels = in_half.shape[2]
+    projected = dot(normed, in_half.reshape(in_half.shape[0], 3 * channels))
+    b_part = projected[:, :channels]
+    c_part = projected[:, channels : 2 * channels]
+    x_part = projected[:, 2 * channels :]
+    mixed = b_part * x_part
+    convolved = jnp.zeros_like(mixed)
+    for k in range(KERNEL):
+        convolved = convolved + kernel_half[k] * shift_down(mixed, KERNEL - 1 - k)
+    gated = (c_part * convolved).astype(BF16)
+    return b_part, c_part, x_part, mixed, convolved, gated
+
+
+def quarter_gather(weight, rows_axis_quarter, dp_index):
+    rows = weight.shape[0] // 4
+    sliced = lax.dynamic_slice_in_dim(weight, rows_axis_quarter * rows, rows, axis=0)
+    first = lax.ppermute(sliced, "tensor", [(0, 1), (1, 0)])
+    n_dp = lax.axis_size("dp")
+    flip_y = [(i, i ^ 2) for i in range(n_dp)]
+    flip_c = [(i, i ^ 1) for i in range(n_dp)]
+    from_y = lax.ppermute(first, "dp", flip_y)
+    both = jnp.stack([first, from_y])
+    from_c = lax.ppermute(both, "dp", flip_c)
+    out = jnp.zeros((4, rows) + weight.shape[1:], weight.dtype)
+    for piece, which in ((both[0], 0), (both[1], 2), (from_c[0], 1), (from_c[1], 3)):
+        out = lax.dynamic_update_slice_in_dim(
+            out, piece[None], rows_axis_quarter ^ which, axis=0
+        )
+    return out.reshape(weight.shape)
+
+
+def fast(
+    block_input,
+    mixer_gain,
+    in_weight,
+    conv_kernel,
+    out_weight,
+    ffn_gain,
+    gate_weight,
+    up_weight,
+    down_weight,
+    output_grad,
+    lengths,
+):
+    rows = block_input.shape[0]
+    channels = in_weight.shape[2]
+    me = lax.axis_index("tensor")
+    dp_index = lax.axis_index("dp")
+    swap = [(0, 1), (1, 0)]
+    quarter = dp_index % 4
+
+    other_input = lax.ppermute(block_input, "tensor", swap)
+    in_other = quarter_gather(in_weight, quarter, dp_index)
+    out_other = quarter_gather(out_weight, quarter, dp_index)
+    kernel_other = lax.ppermute(conv_kernel, "tensor", swap).astype(F32)
+    other_grad = lax.ppermute(output_grad, "tensor", swap)
+    kernel_own = conv_kernel.astype(F32)
+
+    position = jnp.arange(rows, dtype=jnp.int32)
+    mask_own = (position < lengths[me])[:, None]
+    mask_other = (position < lengths[1 - me])[:, None]
+    cot_own = jnp.where(mask_own, output_grad, jnp.zeros_like(output_grad))
+    cot_other = jnp.where(mask_other, other_grad, jnp.zeros_like(other_grad))
+
+    def forward(source_low):
+        source = source_low.astype(F32)
+        normed, inverse = rms_forward(source, mixer_gain)
+        normed = normed.astype(BF16)
+        parts = [
+            mixer_forward(normed, w, k)
+            for w, k in ((in_weight, kernel_own), (in_other, kernel_other))
+        ]
+        hidden = source + (dot(parts[0][5], out_weight) + dot(parts[1][5], out_other))
+        normed_two, inverse_two = rms_forward(hidden, ffn_gain)
+        return source, normed, inverse, parts, hidden, normed_two.astype(BF16), inverse_two
+
+    source, normed_one, inverse_one, parts, hidden, n2_own, inverse_two = forward(block_input)
+    n2_other = forward(other_input)[5]
+
+    inner_o, gg_o, ug_o, out_o, n2g_o = ffn(n2_own, cot_own, gate_weight, up_weight, down_weight, "ffn_own")
+    inner_p, gg_p, ug_p, out_p, n2g_p = ffn(
+        n2_other, cot_other, gate_weight, up_weight, down_weight, "ffn_other"
+    )
+    n2g_recv = lax.ppermute(n2g_p, "tensor", swap)
+    out_recv = lax.ppermute(out_p, "tensor", swap)
+
+    def pair(a_o, a_p, b_o, b_p):
+        return dot(
+            jnp.concatenate([a_o, a_p], axis=0), jnp.concatenate([b_o, b_p], axis=0), TN
+        ).astype(BF16)
+
+    down_grad = pair(inner_o, inner_p, cot_own, cot_other)
+    gate_grad = pair(n2_own, n2_other, gg_o, gg_p)
+    up_grad = pair(n2_own, n2_other, ug_o, ug_p)
+
+    normed_two_grad = n2g_o.astype(F32) + n2g_recv.astype(F32)
+    block_output = (hidden + (out_o.astype(F32) + out_recv.astype(F32))).astype(BF16)
+    through_two, ffn_gain_part = rms_backward(hidden, inverse_two, ffn_gain, normed_two_grad)
+    hidden_grad = cot_own.astype(F32) + through_two
+    hidden_low = hidden_grad.astype(BF16)
+
+    normed_one_grad = 0.0
+    in_grads, out_grads, kernel_grads = [], [], []
+    for half, w_in, w_out, kernel in (
+        (parts[0], in_weight, out_weight, kernel_own),
+        (parts[1], in_other, out_other, kernel_other),
+    ):
+        b_part, c_part, x_part, mixed, convolved, gated = half
+        gated_grad = dot(hidden_low, w_out, NT)
+        out_grads.append(dot(gated, hidden_low, TN).astype(BF16))
+        c_grad = gated_grad * convolved
+        conv_grad = gated_grad * c_part
+        mixed_grad = jnp.zeros_like(conv_grad)
+        kernel_rows = []
+        for k in range(KERNEL):
+            back = KERNEL - 1 - k
+            mixed_grad = mixed_grad + kernel[k] * shift_up(conv_grad, back)
+            kernel_rows.append(jnp.sum(conv_grad * shift_down(mixed, back), axis=0))
+        kernel_grads.append(jnp.stack(kernel_rows))
+        projected_grad = jnp.concatenate(
+            [mixed_grad * x_part, c_grad, mixed_grad * b_part], axis=1
+        ).astype(BF16)
+        w_flat = w_in.reshape(w_in.shape[0], 3 * channels)
+        in_grads.append(dot(normed_one, projected_grad, TN).astype(BF16))
+        normed_one_grad = normed_one_grad + dot(projected_grad, w_flat, NT)
+    through_one, mixer_gain_part = rms_backward(source, inverse_one, mixer_gain, normed_one_grad)
+    input_grad = (hidden_grad + through_one).astype(BF16)
+
+    in_grad = in_grads[0] + lax.ppermute(in_grads[1], "tensor", swap)
+    out_grad = out_grads[0] + lax.ppermute(out_grads[1], "tensor", swap)
+
+    kernel_first = jnp.where(me == 0, kernel_grads[0], kernel_grads[1])
+    kernel_second = jnp.where(me == 0, kernel_grads[1], kernel_grads[0])
+    small = jnp.concatenate(
+        [
+            mixer_gain_part[None],
+            ffn_gain_part[None],
+            jnp.concatenate([kernel_first, kernel_second], axis=1),
+        ],
+        axis=0,
+    )
+    small = lax.psum(small, ("dp", "tensor"))
+    conv_kernel_grad = lax.dynamic_slice_in_dim(small[2:], me * channels, channels, axis=1)
+
+    down_grad, gate_grad, up_grad, in_grad, out_grad = [
+        lax.psum(g, "dp").astype(F32) for g in (down_grad, gate_grad, up_grad, in_grad, out_grad)
+    ]
+    return (
+        block_output,
+        input_grad,
+        small[0],
+        in_grad.reshape(in_weight.shape),
+        conv_kernel_grad,
+        out_grad,
+        small[1],
+        gate_grad,
+        up_grad,
+        down_grad,
+    )
+
+
 def solution(mesh):
+    def step(*args):
+        rows, slots = args[0].shape[0], args[10].shape[0]
+        whole_slots = mesh.shape["tensor"] == 2 and slots == 2 and mesh.shape["dp"] % 4 == 0 and rows == 1024
+        return (fast if whole_slots else local)(*args)
+
     return jax.shard_map(
-        local,
+        step,
         mesh=mesh,
         in_specs=(
             P(("dp", "tensor"), None),

time: 977 us -> 927 us (0.949)
  waiting for transfers between devices: 582 us -> 397 us
  local copies, waits for them, and re-layouts: 13.3 us -> 190 us
  matrix products: 200 us -> 116 us
  Pallas kernels: 0 us -> 75.3 us
  blocking collectives: 73.3 us -> 42 us
  other arithmetic: 84.3 us -> 58.2 us
  starting transfers between devices: 0.54 us -> 15.3 us
    all_gather x4 -> x0, waiting for transfers between devices: 191 us -> none  [the longest x1 56.9 us: local(): lax.all_gather(hidden_grad.astype(jnp.bfloat16), 'tensor', axis=0, tiled=...]
    reduce_scatter x4 -> x0, waiting for transfers between devices: 146 us -> none  [the longest x1 54.4 us: local(): lax.psum_scatter(jnp.dot(gated, out_weight, preferred_element_type=jnp.fl...]
    dynamic_update_slice x0 -> x8, local copies, waits for them, and re-layouts: none -> 133 us  [quarter_gather(): lax.dynamic_update_slice_in_dim(out, piece[None], rows_axis_quarter ^ whi...]
    ppermute x0 -> x13, waiting for transfers between devices: none -> 131 us  [the longest x1 68.8 us: fast(): out_grad = out_grads[0] + lax.ppermute(out_grads[1], 'tensor', swap)]
    dot_general x15 -> x19, matrix products: 200 us -> 116 us  [dot(): return lax.dot_general(a, b, dims, preferred_element_type=F32)]
    pallas_call x0 -> x2, Pallas kernels: none -> 75.3 us  [ffn(): pl.pallas_call(functools.partial(ffn_kernel, rows=256), grid=(hidden // t...]
    psum x2 -> x1, blocking collectives: 73.3 us -> 42 us  [fast(): small = lax.psum(small, ('dp', 'tensor'))]
    psum x1, waiting for transfers between devices: 245 us -> 266 us  [fast(): lax.psum(g, 'dp').astype(F32)]
  transfers between devices with their start and end apart: 9 -> 14, of which waited for: 8 -> 5; matrix products, arithmetic and copies ran while one was open for 13% -> 22% of each run, Pallas kernels for 0% -> 4%
where the time goes in v1:
time: 927 us; the launch traced here: 910 us
  waiting for transfers between devices  397 us (43%)
  local copies, waits for them, and re-layouts  190 us (20%)
  matrix products  116 us (13%)
  Pallas kernels  75.3 us (8%)
  other arithmetic  58.2 us (6%)
  blocking collectives  42 us (5%)
  starting transfers between devices  15.3 us (2%)
  between operations  15 us (2%)
    psum x1, waiting for transfers between devices, fast(): lax.psum(g, 'dp').astype(F32)  266 us
    dynamic_update_slice x8, local copies, waits for them, and re-layouts, quarter_gather(): lax.dynamic_update_slice_in_dim(out, piece[None], rows_axis_quarter ^ whi...  133 us
    dot_general x19, matrix products, dot(): return lax.dot_general(a, b, dims, preferred_element_type=F32)  116 us
    pallas_call x2, Pallas kernels, ffn(): pl.pallas_call(functools.partial(ffn_kernel, rows=256), grid=(hidden // t...  75.3 us
    ppermute x1, waiting for transfers between devices, fast(): out_grad = out_grads[0] + lax.ppermute(out_grads[1], 'tensor', swap)  68.8 us
    ppermute x2, waiting for transfers between devices, quarter_gather(): first = lax.ppermute(sliced, 'tensor', [(0, 1), (1, 0)])  42.3 us
    psum x1, blocking collectives, fast(): small = lax.psum(small, ('dp', 'tensor'))  42 us
    unnamed x105, local copies, waits for them, and re-layouts  22.5 us
  transfers between devices with their start and end apart: 14, of which 5 were waited for; matrix products, arithmetic and copies ran while one was open for 22% of the time, Pallas kernels for 4%

profile of v1, /device:TPU:0, one launch (start us, length us, event | category | flops | bytes accessed | tf_op | source)
XLA Modules:
  0.0 910.3 jit_solution(10179060332196228194)
XLA Ops:
  22.9 5.3 fusion.89
  39.2 42.3 %collective-permute-done.4 = bf16[128,1024]{1,0:T(8,128)(2,1)S(1)} collective-permute-done((bf16[128,1024]{1,0:T(8,128)(2,1)}, bf16[128,1024]{1,0:T(8,128)(2,1)S(1)}, u32[]{:S(2)}, u32[]{:S(2)}) %collective-permute-start.4) | collective-permute-done | bytes 262176 | tf_op jit(solution)/shard_map/ppermute | solution.py:295
  100.7 32.0 %dynamic_update_slice.24 = bf16[4,256,3,512]{1,0,3,2:T(4,128)(2,1)} dynamic-update-slice(bf16[4,256,3,512]{1,0,3,2:T(4,128)(2,1)} %broadcast_in_dim.21, bf16[1,256,3,512]{1,0,3,2:T(2,128)(2,1)} %copy.23, s32[]{:T(128)S(6)} %select_n.59, s32[]{:T(128)} %constant.44.clone.1, s32[]{:T(128)} %constant.44.clone.1, s32[]{:T(128)} %constant.44.clone.1) | dynamic-update-slice | bytes 1572868 | tf_op jit(solution)/shard_map/dynamic_update_slice | solution.py:304
  143.7 32.5 %dynamic_update_slice.25 = bf16[4,256,3,512]{1,0,3,2:T(4,128)(2,1)} dynamic-update-slice(bf16[4,256,3,512]{1,0,3,2:T(4,128)(2,1)} %dynamic_update_slice.24, bf16[1,256,3,512]{1,0,3,2:T(2,128)(2,1)} %copy.24, s32[]{:T(128)S(6)} %select_n.60, s32[]{:T(128)} %constant.44.clone.1, s32[]{:T(128)} %constant.44.clone.1, s32[]{:T(128)} %constant.44.clone.1) | dynamic-update-slice | bytes 1572868 | tf_op jit(solution)/shard_map/dynamic_update_slice | solution.py:304
  178.2 6.0 fusion.72
  203.6 32.0 %dynamic_update_slice.26 = bf16[4,256,3,512]{1,0,3,2:T(4,128)(2,1)} dynamic-update-slice(bf16[4,256,3,512]{1,0,3,2:T(4,128)(2,1)} %dynamic_update_slice.25, bf16[1,256,3,512]{1,0,3,2:T(2,128)(2,1)} %copy.25, s32[]{:T(128)S(6)} %select_n.61, s32[]{:T(128)} %constant.44.clone.1, s32[]{:T(128)} %constant.44.clone.1, s32[]{:T(128)} %constant.44.clone.1) | dynamic-update-slice | bytes 1572868 | tf_op jit(solution)/shard_map/dynamic_update_slice | solution.py:304
  235.6 32.1 %dynamic_update_slice.27 = bf16[4,256,3,512]{1,0,3,2:T(4,128)(2,1)} dynamic-update-slice(bf16[4,256,3,512]{1,0,3,2:T(4,128)(2,1)} %dynamic_update_slice.26, bf16[1,256,3,512]{1,0,3,2:T(2,128)(2,1)} %copy.26, s32[]{:T(128)S(6)} %select_n.62, s32[]{:T(128)} %constant.44.clone.1, s32[]{:T(128)} %constant.44.clone.1, s32[]{:T(128)} %constant.44.clone.1) | dynamic-update-slice | bytes 1572868 | tf_op jit(solution)/shard_map/dynamic_update_slice | solution.py:304
  273.9 6.7 fusion.70
  297.1 37.8 %ffn_other.1 = (bf16[1024,2304]{1,0:T(8,128)(2,1)}, bf16[1024,2304]{1,0:T(8,128)(2,1)}, bf16[1024,2304]{1,0:T(8,128)(2,1)}, bf16[1024,1024]{1,0:T(8,128)(2,1)S(1)}, bf16[1024,1024]{1,0:T(8,128)(2,1)S(1)}) custom-call(bf16[1024,1024]{1,0:T(8,128)(2,1)} %get-tuple-element.81.n2, bf16[1024,1024]{1,0:T(8,128)(2,1)} %broadcast_select_fusion.cot, ...), custom_call_target="tpu_custom_call" | custom-call | flops 28991029248 | bytes 36700160 | tf_op jit(solution)/shard_map/ffn_other/pallas_call | solution.py:252
  336.9 37.5 %ffn_own.1 = (bf16[1024,2304]{1,0:T(8,128)(2,1)}, bf16[1024,2304]{1,0:T(8,128)(2,1)}, bf16[1024,2304]{1,0:T(8,128)(2,1)}, bf16[1024,1024]{1,0:T(8,128)(2,1)S(1)}, bf16[1024,1024]{1,0:T(8,128)(2,1)S(1)}) custom-call(bf16[1024,1024]{1,0:T(8,128)(2,1)} %get-tuple-element.80.n2, bf16[1024,1024]{1,0:T(8,128)(2,1)} %broadcast_select_fusion.1.cot, ...), custom_call_target="tpu_custom_call" | custom-call | flops 28991029248 | bytes 36700160 | tf_op jit(solution)/shard_map/ffn_own/pallas_call | solution.py:252
  374.4 15.7 %fusion.12 = bf16[2304,1024]{1,0:T(8,128)(2,1)} fusion(bf16[1024,2304]{1,0:T(8,128)(2,1)} %get-tuple-element.29, bf16[1024,2304]{1,0:T(8,128)(2,1)} %get-tuple-element.28, bf16[1024,1024]{1,0:T(8,128)(2,1)} %broadcast_select_fusion.cot, bf16[1024,1024]{1,0:T(8,128)(2,1)} %broadcast_select_fusion.1.cot), kind=kOutput, calls=%fused_computation.21 | convolution fusion | flops 9693298688 | bytes 18350080 | tf_op jit(solution)/shard_map/dot_general | solution.py:203
  390.1 16.0 %fusion.15 = bf16[1024,2304]{1,0:T(8,128)(2,1)} fusion(bf16[1024,2304]{1,0:T(8,128)(2,1)} %get-tuple-element.27, bf16[1024,2304]{1,0:T(8,128)(2,1)} %get-tuple-element.26, bf16[1024,1024]{1,0:T(8,128)(2,1)} %get-tuple-element.81.n2, bf16[1024,1024]{1,0:T(8,128)(2,1)} %get-tuple-element.80.n2), kind=kOutput, calls=%fused_computation.22 | convolution fusion | flops 9693298688 | bytes 18350080 | tf_op jit(solution)/shard_map/dot_general | solution.py:203
  409.3 18.4 %collective-permute-done.9 = bf16[1024,1024]{1,0:T(8,128)(2,1)} collective-permute-done((bf16[1024,1024]{1,0:T(8,128)(2,1)S(1)}, bf16[1024,1024]{1,0:T(8,128)(2,1)}, u32[]{:S(2)}, u32[]{:S(2)}) %collective-permute-start.9) | collective-permute-done | bytes 2097184 | tf_op jit(solution)/shard_map/ppermute | solution.py:363
  427.8 6.0 fusion.93
  440.1 5.9 convolution_convert_fusion
  447.5 16.3 %fusion.18 = bf16[1024,2304]{1,0:T(8,128)(2,1)} fusion(bf16[1024,2304]{1,0:T(8,128)(2,1)} %get-tuple-element.25, bf16[1024,2304]{1,0:T(8,128)(2,1)} %get-tuple-element.24, bf16[1024,1024]{1,0:T(8,128)(2,1)} %get-tuple-element.81.n2, bf16[1024,1024]{1,0:T(8,128)(2,1)} %get-tuple-element.80.n2), kind=kOutput, calls=%fused_computation.23 | convolution fusion | flops 9693298688 | bytes 18350080 | tf_op jit(solution)/shard_map/dot_general | solution.py:203
  469.4 68.8 %collective-permute-done.12 = bf16[512,1024]{1,0:T(8,128)(2,1)S(1)} collective-permute-done((bf16[512,1024]{1,0:T(8,128)(2,1)S(1)}, bf16[512,1024]{1,0:T(8,128)(2,1)S(1)}, u32[]{:S(2)}, u32[]{:S(2)}) %collective-permute-start.12) | collective-permute-done | bytes 1048608 | tf_op jit(solution)/shard_map/ppermute | solution.py:408
  540.4 7.3 fusion.38
  552.5 6.1 fusion.59
  558.7 5.7 fusion.33
  564.4 42.0 %psum.42 = f32[5,1024]{1,0:T(8,128)S(1)} all-reduce(f32[5,1024]{1,0:T(8,128)S(1)} %maximum_maximum_fusion), channel_id=1, replica_groups=mesh['dp'=16,'tensor'=2] {'dp','tensor'}, use_global_device_ids=true, to_apply=%region_14.15 | all-reduce | flops 5120 | bytes 40960 | tf_op jit(solution)/shard_map/psum | solution.py:420
  613.0 266.5 %all-reduce.15.cloned.1.call-done = (bf16[1024,3,512]{0,2,1:T(8,128)(2,1)}, bf16[512,1024]{1,0:T(8,128)(2,1)}, bf16[1024,2304]{1,0:T(8,128)(2,1)}, bf16[1024,2304]{1,0:T(8,128)(2,1)}, bf16[2304,1024]{1,0:T(8,128)(2,1)}) async-done(((bf16[1024,3,512]{0,2,1:T(8,128)(2,1)}, bf16[512,1024]{1,0:T(8,128)(2,1)}, bf16[1024,2304]{1,0:T(8,128)(2,1)}, bf16[1024,2304]{1,0:T(8,128)(2,1)}, bf16[2304,1024]{1,0:T(8,128)(2,1)}), ...) | async-done | bytes 18350096 | tf_op jit(solution)/shard_map/psum | solution.py:424
  879.4 7.3 convert_element_type.142
  896.1 5.5 copy.28
  (193 shorter events, 143.5 us)
Async XLA Ops:
  7.2 872.2 %all-reduce.15.cloned.1.call-start = ((), (), s32[]{:S(2)}) async-start(), calls=%async_computation | async-start | bytes 36700160 | tf_op jit(solution)/shard_map/psum | solution.py:424
  9.4 79.6 %collective-permute-start = (bf16[256,3,512]{2,0,1:T(8,128)(2,1)}, bf16[256,3,512]{2,0,1:T(8,128)(2,1)}, u32[]{:S(2)}, u32[]{:S(2)}) collective-permute-start(bf16[256,3,512]{2,0,1:T(8,128)(2,1)} %constant_dynamic-slice_fusion.2), channel_id=1, source_target_pairs={{0,1},{1,0},{2,3},{3,2},{4,5},{5,4},{6,7},{7,6},{8,9},{9,8},{10,11... | collective-permute-start | bytes 2359304 | tf_op jit(solution)/shard_map/ppermute | solution.py:295
  12.3 163.8 %collective-permute-start.7 = (bf16[1024,1024]{1,0:T(8,128)(2,1)}, bf16[1024,1024]{1,0:T(8,128)(2,1)}, u32[]{:S(2)}, u32[]{:S(2)}) collective-permute-start(bf16[1024,1024]{1,0:T(8,128)(2,1)} %param.11), channel_id=1, source_target_pairs={{0,1},{1,0},{2,3},{3,2},{4,5},{5,4},{6,7},{7,6},{8,9},{9,8},{10,11... | collective-permute-start | bytes 6291464 | tf_op jit(solution)/shard_map/ppermute | solution.py:330
  13.1 68.4 %collective-permute-start.4 = (bf16[128,1024]{1,0:T(8,128)(2,1)}, bf16[128,1024]{1,0:T(8,128)(2,1)S(1)}, u32[]{:S(2)}, u32[]{:S(2)}) collective-permute-start(bf16[128,1024]{1,0:T(8,128)(2,1)} %constant_dynamic-slice_fusion.1), channel_id=1, source_target_pairs={{0,1},{1,0},{2,3},{3,2},{4,5},{5,4},{6,7},{7,6},{8,9},{9,8},{10,11... | collective-permute-start | bytes 786440 | tf_op jit(solution)/shard_map/ppermute | solution.py:295
  15.1 73.9 %collective-permute-start.3 = (bf16[3,512]{1,0:T(4,128)(2,1)}, bf16[3,512]{1,0:T(4,128)(2,1)S(1)}, u32[]{:S(2)}, u32[]{:S(2)}) collective-permute-start(bf16[3,512]{1,0:T(4,128)(2,1)} %param.14), channel_id=1, source_target_pairs={{0,1},{1,0},{2,3},{3,2},{4,5},{5,4},{6,7},{7,6},{8,9},{9,8},{10,11... | collective-permute-start | bytes 9224 | tf_op jit(solution)/shard_map/ppermute | solution.py:333
  15.2 169.5 %collective-permute-start.8 = (bf16[1024,1024]{1,0:T(8,128)(2,1)}, bf16[1024,1024]{1,0:T(8,128)(2,1)}, u32[]{:S(2)}, u32[]{:S(2)}) collective-permute-start(bf16[1024,1024]{1,0:T(8,128)(2,1)} %param.20), channel_id=1, source_target_pairs={{0,1},{1,0},{2,3},{3,2},{4,5},{5,4},{6,7},{7,6},{8,9},{9,8},{10,11... | collective-permute-start | bytes 6291464 | tf_op jit(solution)/shard_map/ppermute | solution.py:334
  21.8 166.1 %copy-start.33 = (f32[1,512]{1,0:T(1,128)}, f32[1,512]{1,0:T(1,128)S(1)}, u32[]{:S(2)}) copy-start(f32[1,512]{1,0:T(1,128)S(1)} %get-tuple-element.85) | copy-start | bytes 6148
  21.8 166.1 %copy-start.35 = (f32[1,512]{1,0:T(1,128)}, f32[1,512]{1,0:T(1,128)S(1)}, u32[]{:S(2)}) copy-start(f32[1,512]{1,0:T(1,128)S(1)} %get-tuple-element.86) | copy-start | bytes 6148
  21.8 166.1 %copy-start.37 = (f32[1,512]{1,0:T(1,128)}, f32[1,512]{1,0:T(1,128)S(1)}, u32[]{:S(2)}) copy-start(f32[1,512]{1,0:T(1,128)S(1)} %get-tuple-element.87) | copy-start | bytes 6148
  39.2 49.8 %copy-start.42 = (pred[1024]{0:T(1024)(128)(4,1)}, pred[1024]{0:T(1024)(128)(4,1)S(1)}, u32[]{:S(2)}) copy-start(pred[1024]{0:T(1024)(128)(4,1)S(1)} %iota_compare_fusion.1) | copy-start | bytes 3076
  81.5 6.7 collective-permute-start.5
  89.0 43.7 %collective-permute-start.6 = (bf16[2,128,1024]{2,1,0:T(8,128)(2,1)}, bf16[2,128,1024]{2,1,0:T(8,128)(2,1)}, u32[]{:S(2)}, u32[]{:S(2)}) collective-permute-start(bf16[2,128,1024]{2,1,0:T(8,128)(2,1)} %pad_maximum_fusion.10), channel_id=1, source_target_pairs={{0,2},{2,0},{4,6},{6,4},{8,10},{10,8},{12,14},{14,12},{16,18},{18,... | collective-permute-start | bytes 1572872 | tf_op jit(solution)/shard_map/ppermute | solution.py:301
  89.0 47.0 %collective-permute-start.1 = (bf16[256,3,512]{2,0,1:T(8,128)(2,1)}, bf16[256,3,512]{2,0,1:T(8,128)(2,1)}, u32[]{:S(2)}, u32[]{:S(2)}) collective-permute-start(bf16[256,3,512]{2,0,1:T(8,128)(2,1)} %collective-permute-done), channel_id=1, source_target_pairs={{0,4},{2,6},{4,0},{6,2},{8,12},{10,14},{12,8},{14,10},{16,20},{18,... | collective-permute-start | bytes 2359304 | tf_op jit(solution)/shard_map/ppermute | solution.py:299
  143.4 47.9 %collective-permute-start.2 = (bf16[2,256,3,512]{3,1,2,0:T(8,128)(2,1)}, bf16[2,256,3,512]{3,1,2,0:T(8,128)(2,1)}, u32[]{:S(2)}, u32[]{:S(2)}) collective-permute-start(bf16[2,256,3,512]{3,1,2,0:T(8,128)(2,1)} %pad_maximum_fusion.5), channel_id=1, source_target_pairs={{0,2},{2,0},{4,6},{6,4},{8,10},{10,8},{12,14},{14,12},{16,18},{18,... | collective-permute-start | bytes 4718600 | tf_op jit(solution)/shard_map/ppermute | solution.py:301
  334.9 71.3 %collective-permute-start.10 = (bf16[1024,1024]{1,0:T(8,128)(2,1)S(1)}, bf16[1024,1024]{1,0:T(8,128)(2,1)}, u32[]{:S(2)}, u32[]{:S(2)}) collective-permute-start(bf16[1024,1024]{1,0:T(8,128)(2,1)S(1)} %get-tuple-element.23), channel_id=1, source_target_pairs={{0,1},{1,0},{2,3},{3,2},{4,5},{5,4},{6,7},{7,6},{8,9},{9,8},{10,11... | collective-permute-start | bytes 6291464 | tf_op jit(solution)/shard_map/ppermute | solution.py:362
  336.4 91.4 %collective-permute-start.9 = (bf16[1024,1024]{1,0:T(8,128)(2,1)S(1)}, bf16[1024,1024]{1,0:T(8,128)(2,1)}, u32[]{:S(2)}, u32[]{:S(2)}) collective-permute-start(bf16[1024,1024]{1,0:T(8,128)(2,1)S(1)} %get-tuple-element.21), channel_id=1, source_target_pairs={{0,1},{1,0},{2,3},{3,2},{4,5},{5,4},{6,7},{7,6},{8,9},{9,8},{10,11... | collective-permute-start | bytes 6291464 | tf_op jit(solution)/shard_map/ppermute | solution.py:363
  406.2 27.6 %slice-start.2 = ((s8[6291456]{0:T(1024)(128)(4,1)}), s8[4194304]{0:T(1024)(128)(4,1)S(1)}, s32[]{:S(2)}) async-start(s8[6291456]{0:T(1024)(128)(4,1)} %bitcast.54), calls=%async_computation.3 | async-start | bytes 8388608
  446.0 94.4 %collective-permute-start.11 = (bf16[1024,1536]{1,0:T(8,128)(2,1)}, bf16[1024,1536]{1,0:T(8,128)(2,1)}, u32[]{:S(2)}, u32[]{:S(2)}) collective-permute-start(bf16[1024,1536]{1,0:T(8,128)(2,1)} %convolution_convert_fusion), channel_id=1, source_target_pairs={{0,1},{1,0},{2,3},{3,2},{4,5},{5,4},{6,7},{7,6},{8,9},{9,8},{10,11... | collective-permute-start | bytes 9437192 | tf_op jit(solution)/shard_map/ppermute | solution.py:407
  465.2 73.0 %collective-permute-start.12 = (bf16[512,1024]{1,0:T(8,128)(2,1)S(1)}, bf16[512,1024]{1,0:T(8,128)(2,1)S(1)}, u32[]{:S(2)}, u32[]{:S(2)}) collective-permute-start(bf16[512,1024]{1,0:T(8,128)(2,1)S(1)} %convolution_convert_fusion.2), channel_id=1, source_target_pairs={{0,1},{1,0},{2,3},{3,2},{4,5},{5,4},{6,7},{7,6},{8,9},{9,8},{10,11... | collective-permute-start | bytes 3145736 | tf_op jit(solution)/shard_map/ppermute | solution.py:408
  468.0 72.4 %copy-start.25 = (bf16[1024,512]{1,0:T(8,128)(2,1)}, bf16[1024,512]{1,0:T(8,128)(2,1)S(1)}, u32[]{:S(2)}) copy-start(bf16[1024,512]{1,0:T(8,128)(2,1)S(1)} %get-tuple-element.69) | copy-start | bytes 3145732
  468.8 71.6 %copy-start.31 = (bf16[1024,512]{1,0:T(8,128)(2,1)}, bf16[1024,512]{1,0:T(8,128)(2,1)S(1)}, u32[]{:S(2)}) copy-start(bf16[1024,512]{1,0:T(8,128)(2,1)S(1)} %get-tuple-element.59) | copy-start | bytes 3145732
  468.8 69.4 %copy-start.28 = (bf16[1024,512]{1,0:T(8,128)(2,1)S(1)}, bf16[1024,512]{1,0:T(8,128)(2,1)}, u32[]{:S(2)}) copy-start(bf16[1024,512]{1,0:T(8,128)(2,1)} %copy-done.27) | copy-start | bytes 3145732
  469.4 71.1 %copy-start.26 = (bf16[1024,512]{1,0:T(8,128)(2,1)}, bf16[1024,512]{1,0:T(8,128)(2,1)S(1)}, u32[]{:S(2)}) copy-start(bf16[1024,512]{1,0:T(8,128)(2,1)S(1)} %multiply_convert_fusion.5) | copy-start | bytes 3145732
  558.7 49.0 %copy-start.39 = (f32[1024]{0:T(1024)S(1)}, f32[1024]{0:T(1024)}, u32[]{:S(2)}) copy-start(f32[1024]{0:T(1024)} %get-tuple-element.76) | copy-start | bytes 12292
  (41 other events, 285.3 us)
Sparse Core Ops, SparseCore 0:
  552.5 326.8 all-reduce.14

commit v2 on v1

--- a/solution.py
+++ b/solution.py
@@ -267,6 +267,267 @@
     )(n2, cot, wg, wu, wd)
 
 
+MESH = pl.DeviceIdType.MESH
+
+
+class Cube:
+    def __init__(self, order, rows):
+        me = lax.axis_index("dp")
+        self.tensor = lax.axis_index("tensor")
+        self.partner, self.size, self.mine, self.theirs = [], [], [], []
+        base, size = 0, rows
+        for bit in order:
+            weight = 1 << bit
+            mine = (me // weight) % 2
+            self.partner.append(me + weight - 2 * weight * mine)
+            size //= 2
+            self.size.append(size)
+            self.mine.append(pl.multiple_of(base + mine * size, size))
+            self.theirs.append(pl.multiple_of(base + (1 - mine) * size, size))
+            base = base + mine * size
+        self.stages = len(order)
+
+    def scatter(self, s, j, held, received, send, recv):
+        return pltpu.make_async_remote_copy(
+            src_ref=held.at[j, pl.ds(self.theirs[s], self.size[s])],
+            dst_ref=received[s].at[j],
+            send_sem=send.at[s, j],
+            recv_sem=recv.at[s, j],
+            device_id=(self.partner[s], self.tensor),
+            device_id_type=MESH,
+        )
+
+    def add(self, s, j, held, received):
+        rows = pl.ds(self.mine[s], self.size[s])
+        held[j, rows, :] = (held[j, rows, :].astype(F32) + received[s][j].astype(F32)).astype(BF16)
+
+    def free(self, s, credit):
+        pl.semaphore_signal(
+            credit.at[s], inc=1, device_id=(self.partner[s], self.tensor), device_id_type=MESH
+        )
+
+    def gather(self, s, j, held, send, recv):
+        rows = pl.ds(self.mine[s], self.size[s])
+        slot = 2 * self.stages - 1 - s
+        return pltpu.make_async_remote_copy(
+            src_ref=held.at[j, rows],
+            dst_ref=held.at[j, rows],
+            send_sem=send.at[slot, j],
+            recv_sem=recv.at[slot, j],
+            device_id=(self.partner[s], self.tensor),
+            device_id_type=MESH,
+        )
+
+
+def enter(devices):
+    barrier = pltpu.get_barrier_semaphore()
+    for device in devices:
+        pl.semaphore_signal(barrier, inc=1, device_id=device, device_id_type=MESH)
+    pl.semaphore_wait(barrier, len(devices))
+
+
+TILE = 256
+
+
+def grads_kernel(
+    n2, cot, inner_o, inner_p, gg_o, gg_p, ug_o, ug_p, n2g, out_p,
+    down_out, gate_out, up_out, n2g_recv, out_recv,
+    held, rc, ry, ra, rb, operand, staged, load_sem, store_sem, send, recv, x_send, x_recv, credit,
+):
+    received = (rc, ry, ra, rb)
+    width = n2.shape[1]
+    rows = inner_o.shape[0]
+    per = inner_o.shape[1] // TILE
+    total = 3 * per
+    cube = Cube((0, 1, 2, 3), TILE)
+    other_x = (lax.axis_index("dp"), 1 - lax.axis_index("tensor"))
+    enter([(p, cube.tensor) for p in cube.partner] + [other_x])
+
+    def swap(src, dst, k):
+        return pltpu.make_async_remote_copy(
+            src_ref=src, dst_ref=dst, send_sem=x_send.at[k], recv_sem=x_recv.at[k],
+            device_id=other_x, device_id_type=MESH,
+        )
+
+    swaps = [swap(n2g, n2g_recv, 0), swap(out_p, out_recv, 1)]
+    for one in swaps:
+        one.start()
+
+    pairs = ((inner_o, inner_p), (gg_o, gg_p), (ug_o, ug_p))
+
+    def loads(group, i, slot):
+        cols = pl.ds(pl.multiple_of(i * TILE, TILE), TILE)
+        return [
+            pltpu.make_async_copy(
+                pairs[group][k].at[:, cols], operand.at[slot, pl.ds(k * rows, rows)], load_sem.at[slot, k]
+            )
+            for k in range(2)
+        ]
+
+    for copy in loads(0, 0, 0):
+        copy.start()
+
+    def hand_back(s, j):
+        pl.semaphore_wait(credit.at[s], 1)
+        cube.gather(s, j, held, send, recv).start()
+
+    def to_y(j):
+        cube.scatter(0, j, held, received, send, recv).wait()
+        cube.free(0, credit)
+        cube.add(0, j, held, received)
+        cube.scatter(1, j, held, received, send, recv).start()
+
+    for group in range(3):
+
+        def compute(i, carry, group=group):
+            j = group * per + i
+            slot = j % 2
+            for copy in loads(group, i, slot):
+                copy.wait()
+
+            @pl.when(i + 1 < per)
+            def _():
+                for copy in loads(group, i + 1, 1 - slot):
+                    copy.start()
+
+            if group < 2:
+
+                @pl.when(i + 1 == per)
+                def _():
+                    for copy in loads(group + 1, 0, 1 - slot):
+                        copy.start()
+
+            if group == 0:
+                held[j] = dot(operand[slot], cot[...], TN).astype(BF16)
+            else:
+                product = dot(n2[...], operand[slot], TN).astype(BF16)
+                for k in range(width // TILE):
+                    held[j, :, k * TILE : (k + 1) * TILE] = product[k * TILE : (k + 1) * TILE]
+            cube.scatter(0, j, held, received, send, recv).start()
+
+            @pl.when(j > 0)
+            def _():
+                to_y(j - 1)
+
+            return carry
+
+        lax.fori_loop(0, per, compute, 0)
+    to_y(total - 1)
+
+    def reduce_step(tick, carry):
+        for lag, s in ((0, 2), (1, 3), (2, 4)):
+            j = tick - lag
+
+            @pl.when((j >= 0) & (j < total))
+            def _(j=j, s=s):
+                cube.scatter(s - 1, j, held, received, send, recv).wait()
+                cube.free(s - 1, credit)
+                cube.add(s - 1, j, held, received)
+                if s < 4:
+                    cube.scatter(s, j, held, received, send, recv).start()
+                else:
+                    hand_back(3, j)
+
+        for lag, s in ((3, 3), (4, 2)):
+            j = tick - lag
+
+            @pl.when((j >= 0) & (j < total))
+            def _(j=j, s=s):
+                cube.gather(s, j, held, send, recv).wait()
+                hand_back(s - 1, j)
+
+        return carry
+
+    lax.fori_loop(0, total + 4, reduce_step, 0)
+
+    def stores(group, i, slot):
+        at = pl.ds(pl.multiple_of(i * TILE, TILE), TILE)
+        if group == 0:
+            return [pltpu.make_async_copy(staged.at[slot], down_out.at[at], store_sem.at[slot, 0])]
+        out = gate_out if group == 1 else up_out
+        return [
+            pltpu.make_async_copy(
+                staged.at[slot, :, pl.ds(k * TILE, TILE)],
+                out.at[pl.ds(k * TILE, TILE), at],
+                store_sem.at[slot, k],
+            )
+            for k in range(width // TILE)
+        ]
+
+    cube.gather(1, 0, held, send, recv).wait()
+    hand_back(0, 0)
+    for group in range(3):
+
+        def finish(i, carry, group=group):
+            j = group * per + i
+            slot = i % 2
+
+            @pl.when(j + 1 < total)
+            def _():
+                cube.gather(1, j + 1, held, send, recv).wait()
+                hand_back(0, j + 1)
+
+            cube.gather(0, j, held, send, recv).wait()
+
+            @pl.when(i >= 2)
+            def _():
+                for copy in stores(group, i - 2, slot):
+                    copy.wait()
+
+            staged[slot] = held[j].astype(F32)
+            for copy in stores(group, i, slot):
+                copy.start()
+            return carry
+
+        lax.fori_loop(0, per, finish, 0)
+        for i in (per - 2, per - 1):
+            for copy in stores(group, i, i % 2):
+                copy.wait()
+    for one in swaps:
+        one.wait()
+
+
+def grads(n2, cot, inner, gg, ug, n2g, out_p):
+    width = n2.shape[1]
+    rows, hidden = inner[0].shape
+    total = 3 * hidden // TILE
+    vmem = pl.BlockSpec(memory_space=pltpu.VMEM)
+    hbm = pl.BlockSpec(memory_space=pl.ANY)
+    sizes = (TILE // 2, TILE // 4, TILE // 8, TILE // 16)
+    return pl.pallas_call(
+        grads_kernel,
+        in_specs=[vmem, vmem] + [hbm] * 8,
+        out_specs=[hbm] * 5,
+        out_shape=[
+            jax.ShapeDtypeStruct((hidden, width), F32),
+            jax.ShapeDtypeStruct((width, hidden), F32),
+            jax.ShapeDtypeStruct((width, hidden), F32),
+            jax.ShapeDtypeStruct((rows, width), BF16),
+            jax.ShapeDtypeStruct((rows, width), BF16),
+        ],
+        scratch_shapes=[pltpu.VMEM((total, TILE, width), BF16)]
+        + [pltpu.VMEM((total, size, width), BF16) for size in sizes]
+        + [
+            pltpu.VMEM((2, 2 * rows, TILE), BF16),
+            pltpu.VMEM((2, TILE, width), F32),
+            pltpu.SemaphoreType.DMA((2, 2)),
+            pltpu.SemaphoreType.DMA((2, width // TILE)),
+            pltpu.SemaphoreType.DMA((8, total)),
+            pltpu.SemaphoreType.DMA((8, total)),
+            pltpu.SemaphoreType.DMA((2,)),
+            pltpu.SemaphoreType.DMA((2,)),
+            pltpu.SemaphoreType.REGULAR((4,)),
+        ],
+        name="grads",
+        cost_estimate=pl.CostEstimate(
+            flops=12 * rows * width * hidden, bytes_accessed=20 * hidden * width, transcendentals=0
+        ),
+        compiler_params=pltpu.CompilerParams(
+            collective_id=1, has_side_effects=True, vmem_limit_bytes=60 * 2**20
+        ),
+    )(n2, cot, *inner, *gg, *ug, n2g, out_p)
+
+
 def shift_down(values, amount):
     return jnp.pad(values, ((amount, 0), (0, 0)))[: values.shape[0]]
 
@@ -276,8 +537,8 @@
 
 
 def mixer_forward(normed, in_half, kernel_half):
-    channels = in_half.shape[2]
-    projected = dot(normed, in_half.reshape(in_half.shape[0], 3 * channels))
+    channels = in_half.shape[1] // 3
+    projected = dot(normed, in_half)
     b_part = projected[:, :channels]
     c_part = projected[:, channels : 2 * channels]
     x_part = projected[:, 2 * channels :]
@@ -299,12 +560,10 @@
     from_y = lax.ppermute(first, "dp", flip_y)
     both = jnp.stack([first, from_y])
     from_c = lax.ppermute(both, "dp", flip_c)
-    out = jnp.zeros((4, rows) + weight.shape[1:], weight.dtype)
+    out = weight
     for piece, which in ((both[0], 0), (both[1], 2), (from_c[0], 1), (from_c[1], 3)):
-        out = lax.dynamic_update_slice_in_dim(
-            out, piece[None], rows_axis_quarter ^ which, axis=0
-        )
-    return out.reshape(weight.shape)
+        out = lax.dynamic_update_slice_in_dim(out, piece, (rows_axis_quarter ^ which) * rows, axis=0)
+    return out
 
 
 def fast(
@@ -328,6 +587,8 @@
     quarter = dp_index % 4
 
     other_input = lax.ppermute(block_input, "tensor", swap)
+    in_shape = in_weight.shape
+    in_weight = in_weight.reshape(in_shape[0], 3 * channels)
     in_other = quarter_gather(in_weight, quarter, dp_index)
     out_other = quarter_gather(out_weight, quarter, dp_index)
     kernel_other = lax.ppermute(conv_kernel, "tensor", swap).astype(F32)
@@ -359,17 +620,15 @@
     inner_p, gg_p, ug_p, out_p, n2g_p = ffn(
         n2_other, cot_other, gate_weight, up_weight, down_weight, "ffn_other"
     )
-    n2g_recv = lax.ppermute(n2g_p, "tensor", swap)
-    out_recv = lax.ppermute(out_p, "tensor", swap)
-
-    def pair(a_o, a_p, b_o, b_p):
-        return dot(
-            jnp.concatenate([a_o, a_p], axis=0), jnp.concatenate([b_o, b_p], axis=0), TN
-        ).astype(BF16)
-
-    down_grad = pair(inner_o, inner_p, cot_own, cot_other)
-    gate_grad = pair(n2_own, n2_other, gg_o, gg_p)
-    up_grad = pair(n2_own, n2_other, ug_o, ug_p)
+    down_grad, gate_grad, up_grad, n2g_recv, out_recv = grads(
+        jnp.concatenate([n2_own, n2_other]),
+        jnp.concatenate([cot_own, cot_other]),
+        (inner_o, inner_p),
+        (gg_o, gg_p),
+        (ug_o, ug_p),
+        n2g_p,
+        out_p,
+    )
 
     normed_two_grad = n2g_o.astype(F32) + n2g_recv.astype(F32)
     block_output = (hidden + (out_o.astype(F32) + out_recv.astype(F32))).astype(BF16)
@@ -398,9 +657,8 @@
         projected_grad = jnp.concatenate(
             [mixed_grad * x_part, c_grad, mixed_grad * b_part], axis=1
         ).astype(BF16)
-        w_flat = w_in.reshape(w_in.shape[0], 3 * channels)
         in_grads.append(dot(normed_one, projected_grad, TN).astype(BF16))
-        normed_one_grad = normed_one_grad + dot(projected_grad, w_flat, NT)
+        normed_one_grad = normed_one_grad + dot(projected_grad, w_in, NT)
     through_one, mixer_gain_part = rms_backward(source, inverse_one, mixer_gain, normed_one_grad)
     input_grad = (hidden_grad + through_one).astype(BF16)
 
@@ -420,14 +678,12 @@
     small = lax.psum(small, ("dp", "tensor"))
     conv_kernel_grad = lax.dynamic_slice_in_dim(small[2:], me * channels, channels, axis=1)
 
-    down_grad, gate_grad, up_grad, in_grad, out_grad = [
-        lax.psum(g, "dp").astype(F32) for g in (down_grad, gate_grad, up_grad, in_grad, out_grad)
-    ]
+    in_grad, out_grad = [lax.psum(g, "dp").astype(F32) for g in (in_grad, out_grad)]
     return (
         block_output,
         input_grad,
         small[0],
-        in_grad.reshape(in_weight.shape),
+        in_grad.reshape(in_shape),
         conv_kernel_grad,
         out_grad,
         small[1],
@@ -439,9 +695,8 @@
 
 def solution(mesh):
     def step(*args):
-        rows, slots = args[0].shape[0], args[10].shape[0]
-        whole_slots = mesh.shape["tensor"] == 2 and slots == 2 and mesh.shape["dp"] % 4 == 0 and rows == 1024
-        return (fast if whole_slots else local)(*args)
+        one_slot_each = mesh.shape["tensor"] == 2 and args[10].shape[0] == 2 and mesh.shape["dp"] == 16
+        return (fast if one_slot_each else local)(*args)
 
     return jax.shard_map(
         step,

time: 927 us -> 728 us (0.79)
  waiting for transfers between devices: 397 us -> 195 us
  Pallas kernels: 75.3 us -> 273 us
  local copies, waits for them, and re-layouts: 190 us -> 55 us
  matrix products: 116 us -> 75.8 us
    psum x1, waiting for transfers between devices: 266 us -> 53.5 us  [fast(): lax.psum(g, 'dp').astype(F32)]
    pallas_call x0 -> x1, Pallas kernels: none -> 197 us  [grads(): pl.pallas_call(grads_kernel, in_specs=[vmem, vmem] + [hbm] * 8, out_specs...]
    dynamic_update_slice x8, local copies, waits for them, and re-layouts: 133 us -> 1.67 us  [quarter_gather(): lax.dynamic_update_slice_in_dim(out, piece, (rows_axis_quarter ^ which) *...]
    dot_general x19 -> x16, matrix products: 116 us -> 75.8 us  [dot(): return lax.dot_general(a, b, dims, preferred_element_type=F32)]
    unnamed x105 -> x104, local copies, waits for them, and re-layouts: 22.5 us -> 45.7 us
    ppermute x2 -> x0, waiting for transfers between devices: 18.4 us -> none  [the longest x1 18.4 us: fast(): out_recv = lax.ppermute(out_p, 'tensor', swap)]
    ppermute x2, waiting for transfers between devices: 1.47 us -> 19.8 us  [quarter_gather(): from_y = lax.ppermute(first, 'dp', flip_y)]
    convert_element_type x4 -> x1, other arithmetic: 18.3 us -> 1.57 us  [fast(): lax.psum(g, 'dp').astype(F32)]
  transfers between devices with their start and end apart: 14 -> 12, of which waited for: 5 -> 6; matrix products, arithmetic and copies ran while one was open for 22% -> 11% of each run, Pallas kernels for 4% -> 0%
where the time goes in v2:
time: 728 us; the launch traced here: 718 us
  Pallas kernels  273 us (38%)
  waiting for transfers between devices  195 us (27%)
  matrix products  75.8 us (10%)
  local copies, waits for them, and re-layouts  55 us (8%)
  other arithmetic  50.6 us (7%)
  blocking collectives  39.1 us (5%)
  between operations  15.3 us (2%)
  starting transfers between devices  13.3 us (2%)
    pallas_call x1, Pallas kernels, grads(): pl.pallas_call(grads_kernel, in_specs=[vmem, vmem] + [hbm] * 8, out_specs...  197 us
    pallas_call x2, Pallas kernels, ffn(): pl.pallas_call(functools.partial(ffn_kernel, rows=256), grid=(hidden // t...  76.3 us
    dot_general x16, matrix products, dot(): return lax.dot_general(a, b, dims, preferred_element_type=F32)  75.8 us
    ppermute x1, waiting for transfers between devices, fast(): out_grad = out_grads[0] + lax.ppermute(out_grads[1], 'tensor', swap)  74.8 us
    psum x1, waiting for transfers between devices, fast(): lax.psum(g, 'dp').astype(F32)  53.5 us
    unnamed x104, local copies, waits for them, and re-layouts  45.7 us
    ppermute x2, waiting for transfers between devices, quarter_gather(): first = lax.ppermute(sliced, 'tensor', [(0, 1), (1, 0)])  39.4 us
    psum x1, blocking collectives, fast(): small = lax.psum(small, ('dp', 'tensor'))  39.1 us
  transfers between devices with their start and end apart: 12, of which 6 were waited for; matrix products, arithmetic and copies ran while one was open for 11% of the time, Pallas kernels for 0%

profile of v2, /device:TPU:0, one launch (start us, length us, event | category | flops | bytes accessed | tf_op | source)
XLA Modules:
  0.0 717.7 jit_solution(13964446912419273968)
XLA Ops:
  7.3 4.7 copy.22
  28.3 6.0 fusion.66
  46.7 39.4 %collective-permute-done.4 = bf16[128,1024]{1,0:T(8,128)(2,1)S(1)} collective-permute-done((bf16[128,1024]{1,0:T(8,128)(2,1)}, bf16[128,1024]{1,0:T(8,128)(2,1)S(1)}, u32[]{:S(2)}, u32[]{:S(2)}) %collective-permute-start.4) | collective-permute-done | bytes 262176 | tf_op jit(solution)/shard_map/ppermute | solution.py:556
  96.3 17.0 %collective-permute-done.1 = bf16[256,1536]{0,1:T(8,128)(2,1)S(1)} collective-permute-done((bf16[256,1536]{0,1:T(8,128)(2,1)}, bf16[256,1536]{0,1:T(8,128)(2,1)S(1)}, u32[]{:S(2)}, u32[]{:S(2)}) %collective-permute-start.1) | collective-permute-done | bytes 786464 | tf_op jit(solution)/shard_map/ppermute | solution.py:560
  117.0 5.1 fusion.50
  122.6 7.8 %collective-permute-done.8 = bf16[1024,1024]{1,0:T(8,128)(2,1)} collective-permute-done((bf16[1024,1024]{1,0:T(8,128)(2,1)}, bf16[1024,1024]{1,0:T(8,128)(2,1)}, u32[]{:S(2)}, u32[]{:S(2)}) %collective-permute-start.8) | collective-permute-done | bytes 2097184 | tf_op jit(solution)/shard_map/ppermute | solution.py:595
  136.9 6.2 fusion.64
  143.2 6.6 fusion.48
  165.4 38.0 %ffn_other.1 = (bf16[1024,2304]{1,0:T(8,128)(2,1)}, bf16[1024,2304]{1,0:T(8,128)(2,1)}, bf16[1024,2304]{1,0:T(8,128)(2,1)}, bf16[1024,1024]{1,0:T(8,128)(2,1)S(1)}, bf16[1024,1024]{1,0:T(8,128)(2,1)S(1)}) custom-call(bf16[1024,1024]{1,0:T(8,128)(2,1)} %get-tuple-element.86.n2, bf16[1024,1024]{1,0:T(8,128)(2,1)} %copy-done.26, bf16[1024,2304]{1,0:T(8,128)(2,1)} %wg.3, ...), custom_call_target="tpu_custom_call" | custom-call | flops 28991029248 | bytes 36700160 | tf_op jit(solution)/shard_map/ffn_other/pallas_call | solution.py:252
  204.7 38.3 %ffn_own.1 = (bf16[1024,2304]{1,0:T(8,128)(2,1)}, bf16[1024,2304]{1,0:T(8,128)(2,1)}, bf16[1024,2304]{1,0:T(8,128)(2,1)}, bf16[1024,1024]{1,0:T(8,128)(2,1)S(1)}, bf16[1024,1024]{1,0:T(8,128)(2,1)S(1)}) custom-call(bf16[1024,1024]{1,0:T(8,128)(2,1)} %get-tuple-element.85.n2, bf16[1024,1024]{1,0:T(8,128)(2,1)} %copy-done.24, bf16[1024,2304]{1,0:T(8,128)(2,1)} %wg.3, ...), custom_call_target="tpu_custom_call" | custom-call | flops 28991029248 | bytes 36700160 | tf_op jit(solution)/shard_map/ffn_own/pallas_call | solution.py:252
  245.7 197.0 %grads.1 = (f32[2304,1024]{1,0:T(8,128)}, f32[1024,2304]{1,0:T(8,128)}, f32[1024,2304]{1,0:T(8,128)}, bf16[1024,1024]{1,0:T(8,128)(2,1)}, bf16[1024,1024]{1,0:T(8,128)(2,1)}) custom-call(bf16[2048,1024]{1,0:T(8,128)(2,1)} %pad_maximum_fusion.n2, bf16[2048,1024]{1,0:T(8,128)(2,1)} %pad_maximum_fusion.1.cot, bf16[1024,2304]{1,0:T(8,128)(2,1)} %get-tuple-element.26.inner_o, ...), custom_call_target="tpu_custom_call" | custom-call | flops 28991029248 | bytes 47185920 | tf_op jit(solution)/shard_map/grads/pallas_call | solution.py:497
  442.8 4.4 multiply_reduce_fusion
  447.5 6.4 fusion.70
  458.4 8.1 %convolution_convert_fusion = bf16[1024,1536]{1,0:T(8,128)(2,1)} fusion(bf16[1024,512]{1,0:T(8,128)(2,1)S(1)} %multiply_convert_fusion.2, bf16[1024,512]{1,0:T(8,128)(2,1)S(1)} %get-tuple-element.75, bf16[1024,512]{1,0:T(8,128)(2,1)S(1)} %get-tuple-element.64, bf16[1024,1024]{1,0:T(8,128)(2,1)} %param.11, f32[1024]{0:T(1024)S(1)} %copy-done.42, ...), kind=kOutput, calls=%fused_computation.34 | convolution fusion | flops 3236429824 | bytes 8396800 | tf_op jit(solution)/shard_map/dot_general | solution.py:203
  479.8 5.0 fusion.35
  484.8 74.8 %collective-permute-done.10 = bf16[512,1024]{1,0:T(8,128)(2,1)S(1)} collective-permute-done((bf16[512,1024]{1,0:T(8,128)(2,1)S(1)}, bf16[512,1024]{1,0:T(8,128)(2,1)S(1)}, u32[]{:S(2)}, u32[]{:S(2)}) %collective-permute-start.10) | collective-permute-done | bytes 1048608 | tf_op jit(solution)/shard_map/ppermute | solution.py:666
  561.9 6.8 fusion.14
  573.4 10.1 %fusion.12 = (f32[1024]{0:T(1024)S(1)}, f32[1024]{0:T(1024)S(1)}, f32[1024,1024]{1,0:T(8,128)}) fusion(bf16[1024,1024]{1,0:T(8,128)(2,1)} %param.11, f32[1024]{0:T(1024)S(1)} %get-tuple-element.82, f32[1024]{0:T(1024)S(1)} %copy-done.42, f32[1024,1024]{1,0:T(8,128)} %fusion.35, bf16[1024,1536]{0,1:T(8,128)(2,1)S(1)} %copy-done.32, ...), kind=kOutput, calls=%fused_computation.21 | convolution fusion | flops 3239049216 | bytes 16793600 | tf_op jit(solution)/shard_map/dot_general | solution.py:203
  583.6 39.1 %psum.21 = f32[5,1024]{1,0:T(8,128)S(1)} all-reduce(f32[5,1024]{1,0:T(8,128)S(1)} %maximum_maximum_fusion), channel_id=1, replica_groups=mesh['dp'=16,'tensor'=2] {'dp','tensor'}, use_global_device_ids=true, to_apply=%region_14.15 | all-reduce | flops 5120 | bytes 40960 | tf_op jit(solution)/shard_map/psum | solution.py:678
  623.9 5.7 fusion.9
  629.6 53.5 %all-reduce.15.cloned.1.call-done = (bf16[1024,3,512]{0,2,1:T(8,128)(2,1)}, bf16[512,1024]{1,0:T(8,128)(2,1)}) async-done(((bf16[1024,3,512]{0,2,1:T(8,128)(2,1)}, bf16[512,1024]{1,0:T(8,128)(2,1)}), (bf16[1024,3,512]{0,2,1:T(8,128)(2,1)}, bf16[512,1024]{1,0:T(8,128)(2,1)})) %all-reduce.15.cloned.1.call-update) | async-done | bytes 4194320 | tf_op jit(solution)/shard_map/psum | solution.py:681
  683.1 5.5 copy.24
  690.1 8.4 %copy.38 = f32[1024,2304]{1,0:T(8,128)} copy(f32[1024,2304]{1,0:T(8,128)} %get-tuple-element.117) | data formatting | bytes 18874368
  698.5 8.1 %copy.39 = f32[1024,2304]{1,0:T(8,128)} copy(f32[1024,2304]{1,0:T(8,128)} %get-tuple-element.118) | data formatting | bytes 18874368
  (177 shorter events, 100.3 us)
Async XLA Ops:
  7.2 675.9 %all-reduce.15.cloned.1.call-start = ((), (), s32[]{:S(2)}) async-start(), calls=%async_computation | async-start | bytes 8388608 | tf_op jit(solution)/shard_map/psum | solution.py:681
  7.3 12.5 %copy-start.41 = (bf16[3,512]{1,0:T(4,128)(2,1)S(1)}, bf16[3,512]{1,0:T(4,128)(2,1)}, u32[]{:S(2)}) copy-start(bf16[3,512]{1,0:T(4,128)(2,1)} %param.14) | copy-start | bytes 9220
  14.1 78.9 %collective-permute-start = (bf16[256,1536]{0,1:T(8,128)(2,1)}, bf16[256,1536]{0,1:T(8,128)(2,1)}, u32[]{:S(2)}, u32[]{:S(2)}) collective-permute-start(bf16[256,1536]{0,1:T(8,128)(2,1)} %constant_dynamic-slice_fusion.2), channel_id=1, source_target_pairs={{0,1},{1,0},{2,3},{3,2},{4,5},{5,4},{6,7},{7,6},{8,9},{9,8},{10,11... | collective-permute-start | bytes 2359304 | tf_op jit(solution)/shard_map/ppermute | solution.py:556
  17.0 97.9 %collective-permute-start.7 = (bf16[1024,1024]{1,0:T(8,128)(2,1)}, bf16[1024,1024]{1,0:T(8,128)(2,1)}, u32[]{:S(2)}, u32[]{:S(2)}) collective-permute-start(bf16[1024,1024]{1,0:T(8,128)(2,1)} %param.11), channel_id=1, source_target_pairs={{0,1},{1,0},{2,3},{3,2},{4,5},{5,4},{6,7},{7,6},{8,9},{9,8},{10,11... | collective-permute-start | bytes 6291464 | tf_op jit(solution)/shard_map/ppermute | solution.py:589
  17.7 68.4 %collective-permute-start.4 = (bf16[128,1024]{1,0:T(8,128)(2,1)}, bf16[128,1024]{1,0:T(8,128)(2,1)S(1)}, u32[]{:S(2)}, u32[]{:S(2)}) collective-permute-start(bf16[128,1024]{1,0:T(8,128)(2,1)} %constant_dynamic-slice_fusion.1), channel_id=1, source_target_pairs={{0,1},{1,0},{2,3},{3,2},{4,5},{5,4},{6,7},{7,6},{8,9},{9,8},{10,11... | collective-permute-start | bytes 786440 | tf_op jit(solution)/shard_map/ppermute | solution.py:556
  19.7 73.2 %collective-permute-start.3 = (bf16[3,512]{1,0:T(4,128)(2,1)S(1)}, bf16[3,512]{1,0:T(4,128)(2,1)S(1)}, u32[]{:S(2)}, u32[]{:S(2)}) collective-permute-start(bf16[3,512]{1,0:T(4,128)(2,1)S(1)} %copy-done.41), channel_id=1, source_target_pairs={{0,1},{1,0},{2,3},{3,2},{4,5},{5,4},{6,7},{7,6},{8,9},{9,8},{10,11... | collective-permute-start | bytes 9224 | tf_op jit(solution)/shard_map/ppermute | solution.py:594
  19.8 110.6 %collective-permute-start.8 = (bf16[1024,1024]{1,0:T(8,128)(2,1)}, bf16[1024,1024]{1,0:T(8,128)(2,1)}, u32[]{:S(2)}, u32[]{:S(2)}) collective-permute-start(bf16[1024,1024]{1,0:T(8,128)(2,1)} %param.20), channel_id=1, source_target_pairs={{0,1},{1,0},{2,3},{3,2},{4,5},{5,4},{6,7},{7,6},{8,9},{9,8},{10,11... | collective-permute-start | bytes 6291464 | tf_op jit(solution)/shard_map/ppermute | solution.py:595
  46.7 46.3 %copy-start.19 = (bf16[512,1024]{1,0:T(8,128)(2,1)S(1)}, bf16[512,1024]{1,0:T(8,128)(2,1)}, u32[]{:S(2)}) copy-start(bf16[512,1024]{1,0:T(8,128)(2,1)} %param.15) | copy-start | bytes 3145732
  46.7 48.2 %copy-start.30 = (bf16[1024,1536]{0,1:T(8,128)(2,1)S(1)}, bf16[1024,1536]{0,1:T(8,128)(2,1)}, u32[]{:S(2)}) copy-start(bf16[1024,1536]{0,1:T(8,128)(2,1)} %copy.25) | copy-start | bytes 9437188
  86.1 6.7 collective-permute-start.5
  90.0 42.2 %copy-start.24 = (bf16[1024,1024]{1,0:T(8,128)(2,1)}, bf16[1024,1024]{1,0:T(8,128)(2,1)S(1)}, u32[]{:S(2)}) copy-start(bf16[1024,1024]{1,0:T(8,128)(2,1)S(1)} %broadcast_select_fusion.1.cot) | copy-start | bytes 6291460
  92.8 3.3 collective-permute-start.6
  93.0 20.3 %collective-permute-start.1 = (bf16[256,1536]{0,1:T(8,128)(2,1)}, bf16[256,1536]{0,1:T(8,128)(2,1)S(1)}, u32[]{:S(2)}, u32[]{:S(2)}) collective-permute-start(bf16[256,1536]{0,1:T(8,128)(2,1)} %collective-permute-done), channel_id=1, source_target_pairs={{0,4},{2,6},{4,0},{6,2},{8,12},{10,14},{12,8},{14,10},{16,20},{18,... | collective-permute-start | bytes 2359304 | tf_op jit(solution)/shard_map/ppermute | solution.py:560
  96.3 20.7 %copy-start.16 = (bf16[512,1024]{1,0:T(8,128)(2,1)}, bf16[512,1024]{1,0:T(8,128)(2,1)S(1)}, u32[]{:S(2)}) copy-start(bf16[512,1024]{1,0:T(8,128)(2,1)S(1)} %fusion.52) | copy-start | bytes 3145732
  114.7 22.0 %collective-permute-start.2 = (bf16[2,256,1536]{1,2,0:T(8,128)(2,1)S(1)}, bf16[2,256,1536]{1,2,0:T(8,128)(2,1)S(1)}, u32[]{:S(2)}, u32[]{:S(2)}) collective-permute-start(bf16[2,256,1536]{1,2,0:T(8,128)(2,1)S(1)} %pad_maximum_fusion.4), channel_id=1, source_target_pairs={{0,2},{2,0},{4,6},{6,4},{8,10},{10,8},{12,14},{14,12},{16,18},{18,... | collective-permute-start | bytes 4718600 | tf_op jit(solution)/shard_map/ppermute | solution.py:562
  204.7 38.3 %copy-start.3 = (bf16[1024,1024]{1,0:T(8,128)(2,1)}, bf16[1024,1024]{1,0:T(8,128)(2,1)S(1)}, u32[]{:S(2)}) copy-start(bf16[1024,1024]{1,0:T(8,128)(2,1)S(1)} %get-tuple-element.32.n2g) | copy-start | bytes 6291460
  204.7 38.3 %copy-start.27 = (bf16[1024,1024]{1,0:T(8,128)(2,1)S(1)}, bf16[1024,1024]{1,0:T(8,128)(2,1)}, u32[]{:S(2)}) copy-start(bf16[1024,1024]{1,0:T(8,128)(2,1)} %get-tuple-element.85.n2) | copy-start | bytes 6291460
  204.7 38.3 %copy-start.28 = (bf16[1024,1024]{1,0:T(8,128)(2,1)S(1)}, bf16[1024,1024]{1,0:T(8,128)(2,1)}, u32[]{:S(2)}) copy-start(bf16[1024,1024]{1,0:T(8,128)(2,1)} %get-tuple-element.86.n2) | copy-start | bytes 6291460
  466.5 95.4 %collective-permute-start.9 = (bf16[1024,1536]{1,0:T(8,128)(2,1)}, bf16[1024,1536]{1,0:T(8,128)(2,1)}, u32[]{:S(2)}, u32[]{:S(2)}) collective-permute-start(bf16[1024,1536]{1,0:T(8,128)(2,1)} %convolution_convert_fusion), channel_id=1, source_target_pairs={{0,1},{1,0},{2,3},{3,2},{4,5},{5,4},{6,7},{7,6},{8,9},{9,8},{10,11... | collective-permute-start | bytes 9437192 | tf_op jit(solution)/shard_map/ppermute | solution.py:665
  470.7 88.9 %collective-permute-start.10 = (bf16[512,1024]{1,0:T(8,128)(2,1)S(1)}, bf16[512,1024]{1,0:T(8,128)(2,1)S(1)}, u32[]{:S(2)}, u32[]{:S(2)}) collective-permute-start(bf16[512,1024]{1,0:T(8,128)(2,1)S(1)} %convolution_convert_fusion.2), channel_id=1, source_target_pairs={{0,1},{1,0},{2,3},{3,2},{4,5},{5,4},{6,7},{7,6},{8,9},{9,8},{10,11... | collective-permute-start | bytes 3145736 | tf_op jit(solution)/shard_map/ppermute | solution.py:666
  479.8 79.8 %copy-start.37 = (bf16[1024,512]{1,0:T(8,128)(2,1)S(1)}, bf16[1024,512]{1,0:T(8,128)(2,1)}, u32[]{:S(2)}) copy-start(bf16[1024,512]{1,0:T(8,128)(2,1)} %copy-done.36) | copy-start | bytes 3145732
  573.4 50.5 %copy-start.40 = (f32[1024]{0:T(1024)S(1)}, f32[1024]{0:T(1024)}, u32[]{:S(2)}) copy-start(f32[1024]{0:T(1024)} %get-tuple-element.81) | copy-start | bytes 12292
  690.1 16.5 %slice-start.2 = ((s8[9437184]{0:T(1024)(128)(4,1)}), s8[4194304]{0:T(1024)(128)(4,1)S(1)}, s32[]{:S(2)}) async-start(s8[9437184]{0:T(1024)(128)(4,1)} %bitcast.68), calls=%async_computation.3 | async-start | bytes 8388608
  690.1 16.5 %slice-start.3 = ((s8[9437184]{0:T(1024)(128)(4,1)}), s8[4194304]{0:T(1024)(128)(4,1)S(1)}, s32[]{:S(2)}) async-start(s8[9437184]{0:T(1024)(128)(4,1)} %bitcast.68), calls=%async_computation.4 | async-start | bytes 8388608
  (37 other events, 177.7 us)
Sparse Core Ops, SparseCore 0:
  571.7 111.3 all-reduce.14

commit v3 on v1

--- a/solution.py
+++ b/solution.py
@@ -271,13 +271,9 @@
     return jnp.pad(values, ((amount, 0), (0, 0)))[: values.shape[0]]
 
 
-def shift_up(values, amount):
-    return jnp.pad(values, ((0, amount), (0, 0)))[amount:]
-
-
 def mixer_forward(normed, in_half, kernel_half):
-    channels = in_half.shape[2]
-    projected = dot(normed, in_half.reshape(in_half.shape[0], 3 * channels))
+    channels = in_half.shape[1] // 3
+    projected = dot(normed, in_half)
     b_part = projected[:, :channels]
     c_part = projected[:, channels : 2 * channels]
     x_part = projected[:, 2 * channels :]
@@ -286,7 +282,487 @@
     for k in range(KERNEL):
         convolved = convolved + kernel_half[k] * shift_down(mixed, KERNEL - 1 - k)
     gated = (c_part * convolved).astype(BF16)
-    return b_part, c_part, x_part, mixed, convolved, gated
+    return jnp.concatenate([projected.astype(BF16), convolved.astype(BF16)], axis=1), gated
+
+
+MESH = pl.DeviceIdType.MESH
+TILE = 256
+RING = 4
+
+
+def enter(devices):
+    barrier = pltpu.get_barrier_semaphore()
+    for device in devices:
+        pl.semaphore_signal(barrier, inc=1, device_id=device, device_id_type=MESH)
+    pl.semaphore_wait(barrier, len(devices))
+
+
+def widen(values):
+    return values.astype(F32)
+
+
+def back_kernel(
+    gains, taps,
+    cot_o, cot_p, n2_o, n2_p, inner_o, inner_p, gg_o, gg_p, ug_o, ug_p, n2g_o, n2g_p, out_p,
+    hidden, source, parts_o, parts_p, in_o, in_p, out_w_o, out_w_p, n1, gated_o, gated_p,
+    summed, input_grad, out_recv, small,
+    ring, rc, ry, ra, rb, rx, small_recv, cot, n2, operand, in_w, pg, part, hid, ngo, ngr, src, ig, nxt, kacc,
+    load_sem, fixed_sem, tile_sem, send, recv, local_sem, x_send, x_recv, small_send, small_rsem,
+):
+    width = cot.shape[1]
+    rows = inner_o.shape[0]
+    channels = gated_o.shape[1]
+    ffn_chunks = 3 * inner_o.shape[1] // TILE
+    own_chunks = in_o.shape[1] // TILE + channels // TILE
+    in_chunks = in_o.shape[1] // TILE
+    total = ffn_chunks + own_chunks
+    half = width // 2
+    sizes = (half, half // 2, half // 4, half // 8)
+
+    me = lax.axis_index("dp")
+    tensor = lax.axis_index("tensor")
+    bits = [(me // (1 << k)) % 2 for k in range(4)]
+    peers = [me + (1 << k) - (2 << k) * bits[k] for k in range(4)]
+    enter([(p, tensor) for p in peers] + [(me, 1 - tensor)])
+
+    def peer_copy(src_ref, dst_ref, send_sem, recv_sem, peer):
+        return pltpu.make_async_remote_copy(
+            src_ref=src_ref, dst_ref=dst_ref, send_sem=send_sem, recv_sem=recv_sem,
+            device_id=(peer, tensor), device_id_type=MESH,
+        )
+
+    def x_copy(src_ref, dst_ref, k):
+        return pltpu.make_async_remote_copy(
+            src_ref=src_ref, dst_ref=dst_ref, send_sem=x_send.at[k], recv_sem=x_recv.at[k],
+            device_id=(me, 1 - tensor), device_id_type=MESH,
+        )
+
+    def stage(j, s):
+        if s == 0:
+            return peers[0], pl.multiple_of(bits[0] * half, half), pl.multiple_of(half - bits[0] * half, half)
+        early = SPLIT_LATE(j)
+        first = jnp.where(early, bits[2], bits[1])
+        second = jnp.where(early, bits[1], bits[2])
+        size = sizes[s]
+        if s == 1:
+            base, bit, peer = 0, first, jnp.where(early, peers[2], peers[1])
+        elif s == 2:
+            base, bit, peer = first * sizes[1], second, jnp.where(early, peers[1], peers[2])
+        else:
+            base, bit, peer = first * sizes[1] + second * sizes[2], bits[3], peers[3]
+        return peer, pl.multiple_of(base + bit * size, size), pl.multiple_of(base + size - bit * size, size)
+
+    landing = (None, ry, ra, rb)
+
+    def scatter0(q):
+        peer, _, theirs = stage(0, 0)
+        return peer_copy(
+            ring.at[q % RING, pl.ds(theirs, half)], rc.at[q], send.at[0, q], recv.at[0, q], peer
+        )
+
+    def scatter(s, j):
+        peer, _, theirs = stage(j, s)
+        return peer_copy(
+            rc.at[j, pl.ds(theirs, sizes[s])], landing[s].at[j], send.at[s, j], recv.at[s, j], peer
+        )
+
+    def add(s, j):
+        _, mine, _ = stage(j, s)
+        at = pl.ds(mine, sizes[s])
+        rc[j, at, :] = (widen(rc[j, at, :]) + widen(landing[s][j])).astype(BF16)
+
+    def region(j, s):
+        _, mine, _ = stage(j, s)
+        start = mine if s == 0 else mine + bits[0] * half
+        return summed.at[
+            pl.ds(pl.multiple_of(start, sizes[s]), sizes[s]), pl.ds(pl.multiple_of(j * TILE, TILE), TILE)
+        ]
+
+    def gather(s, j):
+        peer, mine, _ = stage(j, s)
+        src_ref = rc.at[j, pl.ds(mine, sizes[s])] if s == 3 else region(j, s)
+        return peer_copy(src_ref, region(j, s), send.at[7 - s, j], recv.at[7 - s, j], peer)
+
+    def keep(j):
+        _, mine, _ = stage(j, 3)
+        return pltpu.make_async_copy(rc.at[j, pl.ds(mine, sizes[3])], region(j, 3), local_sem.at[j])
+
+    def when(j, what):
+        @pl.when((j >= 0) & (j < total))
+        def _():
+            what()
+
+    def tick(k):
+        for lag, s in ((0, 1), (1, 2), (2, 3)):
+
+            def reduce(j=k - lag, s=s):
+                scatter(s, j).wait()
+                add(s, j)
+                if s < 3:
+                    scatter(s + 1, j).start()
+                else:
+                    gather(3, j).start()
+                    keep(j).start()
+
+            when(k - lag, reduce)
+        for lag, s in ((3, 3), (4, 2)):
+
+            def spread(j=k - lag, s=s):
+                gather(s, j).wait()
+                if s == 3:
+                    keep(j).wait()
+                gather(s - 1, j).start()
+
+            when(k - lag, spread)
+
+    def finish(j):
+        gather(1, j).wait()
+        gather(0, j).start()
+
+        @pl.when(j > 0)
+        def _():
+            gather(0, j - 1).wait()
+
+    def ticks(low, high):
+        def one(k, carry):
+            tick(k)
+            return carry
+
+        lax.fori_loop(low, high, one, 0)
+
+    def fixed(k, src_ref, dst_ref):
+        return pltpu.make_async_copy(src_ref, dst_ref, fixed_sem.at[k])
+
+    first_loads = [fixed(0, cot_o, cot.at[pl.ds(0, rows)]), fixed(1, cot_p, cot.at[pl.ds(rows, rows)])]
+    second_loads = [fixed(2, n2_o, n2.at[pl.ds(0, rows)]), fixed(3, n2_p, n2.at[pl.ds(rows, rows)])]
+    mixer_loads = [fixed(4, in_o, in_w.at[0]), fixed(5, in_p, in_w.at[1])]
+    out_loads = [
+        fixed(6, out_w_o, cot.at[pl.ds(rows, channels)]),
+        fixed(7, out_w_p, cot.at[pl.ds(rows + channels, channels)]),
+    ]
+    late_loads = [fixed(8, n1, n2.at[pl.ds(0, rows)])]
+    gated_loads = [
+        fixed(9, gated_o, n2.at[pl.ds(rows, rows), pl.ds(0, channels)]),
+        fixed(10, gated_p, n2.at[pl.ds(rows, rows), pl.ds(channels, channels)]),
+    ]
+
+    def start(copies):
+        for copy in copies:
+            copy.start()
+
+    def wait(copies):
+        for copy in copies:
+            copy.wait()
+
+    groups = ((inner_o, inner_p), (gg_o, gg_p), (ug_o, ug_p))
+    per = ffn_chunks // 3
+
+    def operands(group, i, slot):
+        cols = pl.ds(pl.multiple_of(i * TILE, TILE), TILE)
+        return [
+            pltpu.make_async_copy(
+                groups[group][k].at[:, cols], operand.at[slot, pl.ds(k * rows, rows)], load_sem.at[slot, k]
+            )
+            for k in range(2)
+        ]
+
+    start(first_loads)
+    start(operands(0, 0, 0))
+    start(second_loads)
+    start(mixer_loads)
+
+    tiles = rows // TILE
+
+    def n2g_block(i):
+        at = pl.ds(pl.multiple_of((tiles - 1 - i) * TILE, TILE), TILE)
+        return x_copy(n2g_p.at[at], ngr.at[at], i)
+
+    for i in range(tiles):
+        n2g_block(i).start()
+    wait(first_loads)
+
+    def from_core(q):
+        scatter0(q).wait()
+        _, mine, _ = stage(0, 0)
+        rc[q] = (widen(ring[q % RING, pl.ds(mine, half), :]) + widen(rc[q])).astype(BF16)
+
+    def to_y(j):
+        from_core(j)
+        scatter(1, j).start()
+
+    for group in range(3):
+        if group == 1:
+            wait(second_loads)
+            start(out_loads)
+
+        def compute(i, carry, group=group):
+            j = group * per + i
+            slot = j % 2
+            wait(operands(group, i, slot))
+
+            @pl.when(i + 1 < per)
+            def _():
+                start(operands(group, i + 1, 1 - slot))
+
+            if group < 2:
+
+                @pl.when(i + 1 == per)
+                def _():
+                    start(operands(group + 1, 0, 1 - slot))
+
+            left = cot if group == 0 else n2
+            ring[j % RING] = dot(left[...], operand[slot], TN).astype(BF16)
+            scatter0(j).start()
+
+            @pl.when(j > 0)
+            def _():
+                to_y(j - 1)
+
+            @pl.when((j >= 8) & (j % 2 == 0))
+            def _():
+                tick((j - 8) // 2)
+
+            return carry
+
+        lax.fori_loop(0, per, compute, 0)
+    start(late_loads)
+    start(gated_loads)
+    to_y(ffn_chunks - 1)
+    done = (ffn_chunks - 1 - 8) // 2 + 1
+
+    nxt[...] = jnp.zeros_like(nxt)
+    kacc[...] = jnp.zeros_like(kacc)
+    small[...] = jnp.zeros_like(small)
+    wait(mixer_loads)
+    wait(out_loads)
+
+    def mixer(i, carry):
+        at = pl.ds(pl.multiple_of((tiles - 1 - i) * TILE, TILE), TILE)
+        loads = [
+            pltpu.make_async_copy(hidden.at[at], hid, tile_sem.at[0]),
+            pltpu.make_async_copy(n2g_o.at[at], ngo, tile_sem.at[1]),
+            pltpu.make_async_copy(source.at[at], src, tile_sem.at[2]),
+            pltpu.make_async_copy(parts_o.at[at], part.at[0], tile_sem.at[3]),
+            pltpu.make_async_copy(parts_p.at[at], part.at[1], tile_sem.at[4]),
+        ]
+        start(loads)
+        n2g_block(i).wait()
+        wait(loads)
+        upstream = widen(ngo[...]) + widen(ngr[at, :])
+        values = hid[...]
+        inverse = lax.rsqrt(jnp.mean(values * values, axis=-1, keepdims=True) + eps)
+        weighted = upstream * gains[1:2, :]
+        scaled = values * inverse
+        small[1:2, :] += jnp.sum(upstream * scaled, axis=0, keepdims=True)
+        along = jnp.mean(weighted * scaled, axis=-1, keepdims=True)
+        grad = widen(cot[at, :]) + inverse * (weighted - scaled * along)
+        grad_low = grad.astype(BF16)
+        cot[at, :] = grad_low
+        row = lax.broadcasted_iota(jnp.int32, (TILE, channels), 0)
+        upstream_one = jnp.zeros((TILE, width), F32)
+        for h in range(2):
+            out_w = cot[pl.ds(rows + h * channels, channels), :]
+            gated_grad = dot(grad_low, out_w, NT)
+            b_part = widen(part[h, :, 0:channels])
+            c_part = widen(part[h, :, channels : 2 * channels])
+            x_part = widen(part[h, :, 2 * channels : 3 * channels])
+            convolved = widen(part[h, :, 3 * channels : 4 * channels])
+            conv_grad = gated_grad * c_part
+            one = jnp.where(row == TILE - 1, nxt[h, 0:1, :], pltpu.roll(conv_grad, TILE - 1, 0))
+            two = jnp.where(
+                row == TILE - 1,
+                nxt[h, 1:2, :],
+                jnp.where(row == TILE - 2, nxt[h, 0:1, :], pltpu.roll(conv_grad, TILE - 2, 0)),
+            )
+            nxt[h, 0:2, :] = conv_grad[0:2, :]
+            mixed_grad = taps[h, 2:3, :] * conv_grad + taps[h, 1:2, :] * one + taps[h, 0:1, :] * two
+            mixed = b_part * x_part
+            kacc[h, 0:1, :] += jnp.sum(mixed * two, axis=0, keepdims=True)
+            kacc[h, 1:2, :] += jnp.sum(mixed * one, axis=0, keepdims=True)
+            kacc[h, 2:3, :] += jnp.sum(mixed * conv_grad, axis=0, keepdims=True)
+            low = jnp.concatenate(
+                [mixed_grad * x_part, gated_grad * convolved, mixed_grad * b_part], axis=1
+            ).astype(BF16)
+            pg[h, at, :] = low
+            upstream_one = upstream_one + dot(low, in_w[h], NT)
+        values_one = widen(src[...])
+        inverse_one = lax.rsqrt(jnp.mean(values_one * values_one, axis=-1, keepdims=True) + eps)
+        weighted_one = upstream_one * gains[0:1, :]
+        scaled_one = values_one * inverse_one
+        small[0:1, :] += jnp.sum(upstream_one * scaled_one, axis=0, keepdims=True)
+        along_one = jnp.mean(weighted_one * scaled_one, axis=-1, keepdims=True)
+        ig[...] = (grad + inverse_one * (weighted_one - scaled_one * along_one)).astype(BF16)
+        store = pltpu.make_async_copy(ig, input_grad.at[at], tile_sem.at[5])
+        store.start()
+        for k in range(3):
+            tick(done + 3 * i + k)
+        store.wait()
+        return carry
+
+    lax.fori_loop(0, tiles, mixer, 0)
+    done = done + 3 * tiles
+    wait(late_loads)
+    wait(gated_loads)
+
+    def piece(h, m_in, m_out):
+        if m_in is not None:
+            cols = pl.ds(pl.multiple_of(m_in * TILE, TILE), TILE)
+            return dot(n2[0:rows, :], pg[h, :, cols], TN)
+        cols = pl.ds(pl.multiple_of(h * channels + m_out * TILE, TILE), TILE)
+        return dot(cot[0:rows, :], n2[rows : 2 * rows, cols], TN)
+
+    def cross(m):
+        return x_copy(rc.at[total + m], rx.at[m], tiles + m)
+
+    def after_core(h, m):
+        if h == 1:
+            from_core(total + m)
+            cross(m).start()
+        else:
+            from_core(ffn_chunks + m)
+
+    for h in (1, 0):
+        base = total if h == 1 else ffn_chunks
+
+        def in_piece(m, carry, h=h, base=base):
+            q = base + m
+            ring[q % RING] = piece(h, m, None).astype(BF16)
+            scatter0(q).start()
+
+            @pl.when(m > 0)
+            def _():
+                after_core(h, m - 1)
+
+            if h == 0:
+
+                @pl.when(done + m < ffn_chunks)
+                def _():
+                    tick(done + m)
+
+            return carry
+
+        lax.fori_loop(0, in_chunks, in_piece, 0)
+        for m in range(in_chunks, own_chunks):
+            ring[(base + m) % RING] = piece(h, None, m - in_chunks).astype(BF16)
+            scatter0(base + m).start()
+            after_core(h, m - 1)
+        after_core(h, own_chunks - 1)
+    last_swap = x_copy(out_p, out_recv, tiles + own_chunks)
+    last_swap.start()
+
+    for h in range(2):
+        cols = pl.ds(pl.multiple_of(channels * (tensor + h - 2 * tensor * h), channels), channels)
+        small[2:5, cols] = kacc[h, 0:3, :]
+
+    def small_copy(k):
+        device = (peers[k], tensor) if k < 4 else (me, 1 - tensor)
+        return pltpu.make_async_remote_copy(
+            src_ref=small, dst_ref=small_recv.at[k], send_sem=small_send.at[k], recv_sem=small_rsem.at[k],
+            device_id=device, device_id_type=MESH,
+        )
+
+    def crossed(m, carry):
+        cross(m).wait()
+        j = ffn_chunks + m
+        rc[j] = (widen(rc[j]) + widen(rx[m])).astype(BF16)
+        scatter(1, j).start()
+        finish(2 * m)
+        finish(2 * m + 1)
+        return carry
+
+    lax.fori_loop(0, own_chunks, crossed, 0)
+    for k in range(5):
+        small_copy(k).start()
+        small_copy(k).wait()
+        small[...] = small[...] + small_recv[k]
+
+    first = 2 * own_chunks
+    lead = 7
+
+    def middle(j, carry):
+        finish(j)
+        return carry
+
+    lax.fori_loop(first, ffn_chunks - lead, middle, 0)
+
+    def drain(k, carry):
+        tick(k)
+        finish(k - lead)
+        return carry
+
+    lax.fori_loop(ffn_chunks, total + 4, drain, 0)
+    lax.fori_loop(total + 4 - lead, total, middle, 0)
+    gather(0, total - 1).wait()
+    last_swap.wait()
+
+
+def back(gains, taps, arrays, rows, width, hidden, channels):
+    ffn_chunks = 3 * hidden // TILE
+    own_chunks = 4 * channels // TILE
+    total = ffn_chunks + own_chunks
+    half = width // 2
+    vmem = pl.BlockSpec(memory_space=pltpu.VMEM)
+    hbm = pl.BlockSpec(memory_space=pl.ANY)
+
+    def buffer(count, size):
+        return pltpu.VMEM((count, size, TILE), BF16)
+
+    return pl.pallas_call(
+        back_kernel,
+        in_specs=[vmem, vmem] + [hbm] * len(arrays),
+        out_specs=[hbm, hbm, hbm, vmem],
+        out_shape=[
+            jax.ShapeDtypeStruct((width, total * TILE), BF16),
+            jax.ShapeDtypeStruct((rows, width), BF16),
+            jax.ShapeDtypeStruct((rows, width), BF16),
+            jax.ShapeDtypeStruct((8, width), F32),
+        ],
+        scratch_shapes=[
+            buffer(RING, width),
+            buffer(total + own_chunks, half),
+            buffer(total, half // 2),
+            buffer(total, half // 4),
+            buffer(total, half // 8),
+            buffer(own_chunks, half),
+            pltpu.VMEM((5, 8, width), F32),
+            pltpu.VMEM((2 * rows, width), BF16),
+            pltpu.VMEM((2 * rows, width), BF16),
+            buffer(2, 2 * rows),
+            pltpu.VMEM((2, width, 3 * channels), BF16),
+            pltpu.VMEM((2, rows, 3 * channels), BF16),
+            pltpu.VMEM((2, TILE, 4 * channels), BF16),
+            pltpu.VMEM((TILE, width), F32),
+            pltpu.VMEM((TILE, width), BF16),
+            pltpu.VMEM((rows, width), BF16),
+            pltpu.VMEM((TILE, width), BF16),
+            pltpu.VMEM((TILE, width), BF16),
+            pltpu.VMEM((2, 8, channels), F32),
+            pltpu.VMEM((2, 8, channels), F32),
+            pltpu.SemaphoreType.DMA((2, 2)),
+            pltpu.SemaphoreType.DMA((11,)),
+            pltpu.SemaphoreType.DMA((6,)),
+            pltpu.SemaphoreType.DMA((8, total + own_chunks)),
+            pltpu.SemaphoreType.DMA((8, total + own_chunks)),
+            pltpu.SemaphoreType.DMA((total,)),
+            pltpu.SemaphoreType.DMA((rows // TILE + own_chunks + 1,)),
+            pltpu.SemaphoreType.DMA((rows // TILE + own_chunks + 1,)),
+            pltpu.SemaphoreType.DMA((5,)),
+            pltpu.SemaphoreType.DMA((5,)),
+        ],
+        name="back",
+        cost_estimate=pl.CostEstimate(
+            flops=12 * rows * width * hidden + 32 * rows * width * channels,
+            bytes_accessed=20 * hidden * width,
+            transcendentals=0,
+        ),
+        compiler_params=pltpu.CompilerParams(
+            collective_id=1, has_side_effects=True, vmem_limit_bytes=63 * 2**20
+        ),
+    )(gains, taps, *arrays)
+
+
+def SPLIT_LATE(j):
+    return j < 0
 
 
 def quarter_gather(weight, rows_axis_quarter, dp_index):
@@ -299,12 +775,10 @@
     from_y = lax.ppermute(first, "dp", flip_y)
     both = jnp.stack([first, from_y])
     from_c = lax.ppermute(both, "dp", flip_c)
-    out = jnp.zeros((4, rows) + weight.shape[1:], weight.dtype)
+    out = weight
     for piece, which in ((both[0], 0), (both[1], 2), (from_c[0], 1), (from_c[1], 3)):
-        out = lax.dynamic_update_slice_in_dim(
-            out, piece[None], rows_axis_quarter ^ which, axis=0
-        )
-    return out.reshape(weight.shape)
+        out = lax.dynamic_update_slice_in_dim(out, piece, (rows_axis_quarter ^ which) * rows, axis=0)
+    return out
 
 
 def fast(
@@ -328,6 +802,8 @@
     quarter = dp_index % 4
 
     other_input = lax.ppermute(block_input, "tensor", swap)
+    in_shape = in_weight.shape
+    in_weight = in_weight.reshape(in_shape[0], 3 * channels)
     in_other = quarter_gather(in_weight, quarter, dp_index)
     out_other = quarter_gather(out_weight, quarter, dp_index)
     kernel_other = lax.ppermute(conv_kernel, "tensor", swap).astype(F32)
@@ -342,106 +818,59 @@
 
     def forward(source_low):
         source = source_low.astype(F32)
-        normed, inverse = rms_forward(source, mixer_gain)
+        normed = rms_forward(source, mixer_gain)[0]
         normed = normed.astype(BF16)
         parts = [
             mixer_forward(normed, w, k)
             for w, k in ((in_weight, kernel_own), (in_other, kernel_other))
         ]
-        hidden = source + (dot(parts[0][5], out_weight) + dot(parts[1][5], out_other))
-        normed_two, inverse_two = rms_forward(hidden, ffn_gain)
-        return source, normed, inverse, parts, hidden, normed_two.astype(BF16), inverse_two
-
-    source, normed_one, inverse_one, parts, hidden, n2_own, inverse_two = forward(block_input)
-    n2_other = forward(other_input)[5]
+        hidden = source + (dot(parts[0][1], out_weight) + dot(parts[1][1], out_other))
+        normed_two = rms_forward(hidden, ffn_gain)[0]
+        return normed, parts, hidden, normed_two.astype(BF16)
+
+    normed_one, parts, hidden, n2_own = forward(block_input)
+    n2_other = forward(other_input)[3]
 
     inner_o, gg_o, ug_o, out_o, n2g_o = ffn(n2_own, cot_own, gate_weight, up_weight, down_weight, "ffn_own")
     inner_p, gg_p, ug_p, out_p, n2g_p = ffn(
         n2_other, cot_other, gate_weight, up_weight, down_weight, "ffn_other"
     )
-    n2g_recv = lax.ppermute(n2g_p, "tensor", swap)
-    out_recv = lax.ppermute(out_p, "tensor", swap)
-
-    def pair(a_o, a_p, b_o, b_p):
-        return dot(
-            jnp.concatenate([a_o, a_p], axis=0), jnp.concatenate([b_o, b_p], axis=0), TN
-        ).astype(BF16)
-
-    down_grad = pair(inner_o, inner_p, cot_own, cot_other)
-    gate_grad = pair(n2_own, n2_other, gg_o, gg_p)
-    up_grad = pair(n2_own, n2_other, ug_o, ug_p)
-
-    normed_two_grad = n2g_o.astype(F32) + n2g_recv.astype(F32)
-    block_output = (hidden + (out_o.astype(F32) + out_recv.astype(F32))).astype(BF16)
-    through_two, ffn_gain_part = rms_backward(hidden, inverse_two, ffn_gain, normed_two_grad)
-    hidden_grad = cot_own.astype(F32) + through_two
-    hidden_low = hidden_grad.astype(BF16)
-
-    normed_one_grad = 0.0
-    in_grads, out_grads, kernel_grads = [], [], []
-    for half, w_in, w_out, kernel in (
-        (parts[0], in_weight, out_weight, kernel_own),
-        (parts[1], in_other, out_other, kernel_other),
-    ):
-        b_part, c_part, x_part, mixed, convolved, gated = half
-        gated_grad = dot(hidden_low, w_out, NT)
-        out_grads.append(dot(gated, hidden_low, TN).astype(BF16))
-        c_grad = gated_grad * convolved
-        conv_grad = gated_grad * c_part
-        mixed_grad = jnp.zeros_like(conv_grad)
-        kernel_rows = []
-        for k in range(KERNEL):
-            back = KERNEL - 1 - k
-            mixed_grad = mixed_grad + kernel[k] * shift_up(conv_grad, back)
-            kernel_rows.append(jnp.sum(conv_grad * shift_down(mixed, back), axis=0))
-        kernel_grads.append(jnp.stack(kernel_rows))
-        projected_grad = jnp.concatenate(
-            [mixed_grad * x_part, c_grad, mixed_grad * b_part], axis=1
-        ).astype(BF16)
-        w_flat = w_in.reshape(w_in.shape[0], 3 * channels)
-        in_grads.append(dot(normed_one, projected_grad, TN).astype(BF16))
-        normed_one_grad = normed_one_grad + dot(projected_grad, w_flat, NT)
-    through_one, mixer_gain_part = rms_backward(source, inverse_one, mixer_gain, normed_one_grad)
-    input_grad = (hidden_grad + through_one).astype(BF16)
-
-    in_grad = in_grads[0] + lax.ppermute(in_grads[1], "tensor", swap)
-    out_grad = out_grads[0] + lax.ppermute(out_grads[1], "tensor", swap)
-
-    kernel_first = jnp.where(me == 0, kernel_grads[0], kernel_grads[1])
-    kernel_second = jnp.where(me == 0, kernel_grads[1], kernel_grads[0])
-    small = jnp.concatenate(
-        [
-            mixer_gain_part[None],
-            ffn_gain_part[None],
-            jnp.concatenate([kernel_first, kernel_second], axis=1),
-        ],
-        axis=0,
-    )
-    small = lax.psum(small, ("dp", "tensor"))
-    conv_kernel_grad = lax.dynamic_slice_in_dim(small[2:], me * channels, channels, axis=1)
-
-    down_grad, gate_grad, up_grad, in_grad, out_grad = [
-        lax.psum(g, "dp").astype(F32) for g in (down_grad, gate_grad, up_grad, in_grad, out_grad)
-    ]
+    width, hidden_units = gate_weight.shape
+    summed, input_grad, out_recv, small = back(
+        jnp.stack([mixer_gain, ffn_gain]),
+        jnp.stack([kernel_own, kernel_other]),
+        (
+            cot_own, cot_other, n2_own, n2_other, inner_o, inner_p, gg_o, gg_p, ug_o, ug_p, n2g_o, n2g_p, out_p,
+            hidden, block_input, parts[0][0], parts[1][0], in_weight, in_other, out_weight, out_other,
+            normed_one, parts[0][1], parts[1][1],
+        ),
+        rows,
+        width,
+        hidden_units,
+        channels,
+    )
+    block_output = (hidden + (widen(out_o) + widen(out_recv))).astype(BF16)
+    conv_kernel_grad = lax.dynamic_slice_in_dim(small[2 : 2 + KERNEL], me * channels, channels, axis=1)
+    splits = [hidden_units, 2 * hidden_units, 3 * hidden_units, 3 * hidden_units + 3 * channels]
+    down_grad, gate_grad, up_grad, in_grad, out_grad = jnp.split(summed, splits, axis=1)
     return (
         block_output,
         input_grad,
         small[0],
-        in_grad.reshape(in_weight.shape),
+        widen(in_grad).reshape(in_shape),
         conv_kernel_grad,
-        out_grad,
+        widen(out_grad.T),
         small[1],
-        gate_grad,
-        up_grad,
-        down_grad,
+        widen(gate_grad),
+        widen(up_grad),
+        widen(down_grad.T),
     )
 
 
 def solution(mesh):
     def step(*args):
-        rows, slots = args[0].shape[0], args[10].shape[0]
-        whole_slots = mesh.shape["tensor"] == 2 and slots == 2 and mesh.shape["dp"] % 4 == 0 and rows == 1024
-        return (fast if whole_slots else local)(*args)
+        one_slot_each = mesh.shape["tensor"] == 2 and args[10].shape[0] == 2 and mesh.shape["dp"] == 16
+        return (fast if one_slot_each else local)(*args)
 
     return jax.shard_map(
         step,

time: 927 us -> 609 us (0.66)
  waiting for transfers between devices: 397 us -> 86.6 us
  Pallas kernels: 75.3 us -> 361 us
  local copies, waits for them, and re-layouts: 190 us -> 60.6 us
  matrix products: 116 us -> 27.2 us
  blocking collectives: 42 us -> 0 us
  between operations: 15 us -> 1.54 us
    pallas_call x0 -> x1, Pallas kernels: none -> 286 us  [back(): pl.pallas_call(back_kernel, in_specs=[vmem, vmem] + [hbm] * len(arrays),...]
    psum x1 -> x0, waiting for transfers between devices: 266 us -> none  [fast(): lax.psum(g, 'dp').astype(F32)]
    dynamic_update_slice x8, local copies, waits for them, and re-layouts: 133 us -> 2.34 us  [quarter_gather(): lax.dynamic_update_slice_in_dim(out, piece, (rows_axis_quarter ^ which) *...]
    dot_general x19 -> x8, matrix products: 116 us -> 27.2 us  [dot(): return lax.dot_general(a, b, dims, preferred_element_type=F32)]
    ppermute x4 -> x0, waiting for transfers between devices: 87.2 us -> none  [the longest x1 68.8 us: fast(): out_grad = out_grads[0] + lax.ppermute(out_grads[1], 'tensor', swap)]
    psum x1 -> x0, blocking collectives: 42 us -> none  [fast(): small = lax.psum(small, ('dp', 'tensor'))]
    ppermute x2, waiting for transfers between devices: 42.3 us -> 66.9 us  [quarter_gather(): first = lax.ppermute(sliced, 'tensor', [(0, 1), (1, 0)])]
    ppermute x2, waiting for transfers between devices: 1.47 us -> 19.7 us  [quarter_gather(): from_y = lax.ppermute(first, 'dp', flip_y)]
  transfers between devices with their start and end apart: 14 -> 9, of which waited for: 5 -> 3; matrix products, arithmetic and copies ran while one was open for 22% -> 9% of each run, Pallas kernels for 4% -> 0%
where the time goes in v3:
time: 609 us; the launch traced here: 599 us
  Pallas kernels  361 us (59%)
  waiting for transfers between devices  86.6 us (14%)
  local copies, waits for them, and re-layouts  60.6 us (10%)
  other arithmetic  51.6 us (8%)
  matrix products  27.2 us (4%)
  starting transfers between devices  10.2 us (2%)
    pallas_call x1, Pallas kernels, back(): pl.pallas_call(back_kernel, in_specs=[vmem, vmem] + [hbm] * len(arrays),...  286 us
    pallas_call x2, Pallas kernels, ffn(): pl.pallas_call(functools.partial(ffn_kernel, rows=256), grid=(hidden // t...  75.2 us
    ppermute x2, waiting for transfers between devices, quarter_gather(): first = lax.ppermute(sliced, 'tensor', [(0, 1), (1, 0)])  66.9 us
    unnamed x55, local copies, waits for them, and re-layouts  39.7 us
    dot_general x8, matrix products, dot(): return lax.dot_general(a, b, dims, preferred_element_type=F32)  27.2 us
    ppermute x2, waiting for transfers between devices, quarter_gather(): from_y = lax.ppermute(first, 'dp', flip_y)  19.7 us
    convert_element_type x2, other arithmetic, widen(): return values.astype(F32)  14.8 us
  transfers between devices with their start and end apart: 9, of which 3 were waited for; matrix products, arithmetic and copies ran while one was open for 9% of the time, Pallas kernels for 0%

profile of v3, /device:TPU:0, one launch (start us, length us, event | category | flops | bytes accessed | tf_op | source)
XLA Modules:
  0.0 598.7 jit_solution(7494452335796060821)
XLA Ops:
  0.6 3.0 collective-permute-start.3
  7.4 4.6 copy.29
  12.0 4.8 copy.31.in_o
  22.7 3.1 broadcast_select_fusion.1.cot.cot_o
  27.7 3.5 fusion.55
  33.6 3.3 fusion.57
  42.0 3.8 copy.45
  47.3 5.1 collective-permute-done.5
  53.2 66.9 %collective-permute-done = bf16[256,1536]{1,0:T(8,128)(2,1)} collective-permute-done((bf16[256,1536]{1,0:T(8,128)(2,1)}, bf16[256,1536]{1,0:T(8,128)(2,1)}, u32[]{:S(2)}, u32[]{:S(2)}) %collective-permute-start) | collective-permute-done | bytes 786464 | tf_op jit(solution)/shard_map/ppermute | solution.py:771
  123.8 14.6 %collective-permute-done.1 = bf16[256,1536]{1,0:T(8,128)(2,1)S(1)} collective-permute-done((bf16[256,1536]{1,0:T(8,128)(2,1)}, bf16[256,1536]{1,0:T(8,128)(2,1)S(1)}, u32[]{:S(2)}, u32[]{:S(2)}) %collective-permute-start.1) | collective-permute-done | bytes 786464 | tf_op jit(solution)/shard_map/ppermute | solution.py:775
  142.1 5.1 fusion.41
  147.8 3.2 broadcast_select_fusion.cot.cot_p
  154.5 3.4 fusion.56
  158.0 5.1 fusion.39
  163.6 3.4 multiply_reduce_fusion
  177.5 37.7 %ffn_other.1 = (bf16[1024,2304]{1,0:T(8,128)(2,1)}, bf16[1024,2304]{1,0:T(8,128)(2,1)}, bf16[1024,2304]{1,0:T(8,128)(2,1)}, bf16[1024,1024]{1,0:T(8,128)(2,1)S(1)}, bf16[1024,1024]{1,0:T(8,128)(2,1)S(1)}) custom-call(bf16[1024,1024]{1,0:T(8,128)(2,1)} %get-tuple-element.67.n2.n2_p, bf16[1024,1024]{1,0:T(8,128)(2,1)} %broadcast_select_fusion.cot.cot_p, ...), custom_call_target="tpu_custom_call" | custom-call | flops 28991029248 | bytes 36700160 | tf_op jit(solution)/shard_map/ffn_other/pallas_call | solution.py:252
  217.9 37.5 %ffn_own.1 = (bf16[1024,2304]{1,0:T(8,128)(2,1)}, bf16[1024,2304]{1,0:T(8,128)(2,1)}, bf16[1024,2304]{1,0:T(8,128)(2,1)}, bf16[1024,1024]{1,0:T(8,128)(2,1)S(1)}, bf16[1024,1024]{1,0:T(8,128)(2,1)S(1)}) custom-call(bf16[1024,1024]{1,0:T(8,128)(2,1)} %get-tuple-element.68.n2.n2_o, bf16[1024,1024]{1,0:T(8,128)(2,1)} %broadcast_select_fusion.1.cot.cot_o, ...), custom_call_target="tpu_custom_call" | custom-call | flops 28991029248 | bytes 36700160 | tf_op jit(solution)/shard_map/ffn_own/pallas_call | solution.py:252
  258.1 285.7 %back.1 = (bf16[1024,8960]{1,0:T(8,128)(2,1)}, bf16[1024,1024]{1,0:T(8,128)(2,1)}, bf16[1024,1024]{1,0:T(8,128)(2,1)}, f32[8,1024]{1,0:T(8,128)}) custom-call(f32[2,1024]{1,0:T(2,128)} %pad_maximum_fusion.5.gains, f32[2,3,512]{2,1,0:T(4,128)} %pad_maximum_fusion.4.taps, bf16[1024,1024]{1,0:T(8,128)(2,1)} %broadcast_select_fusion.1.cot.cot_o, ...), custom_call_target="tpu_custom_call" | custom-call | flops 46170898432 | bytes 47185920 | tf_op jit(solution)/shard_map/back/pallas_call | solution.py:710
  547.5 5.5 slice_convert_fusion.2
  553.0 13.3 %convert_bitcast_fusion = (f32[2304,1024]{0,1:T(8,128)}, f32[1024,2304]{1,0:T(8,128)}, f32[1024,2304]{1,0:T(8,128)}) fusion(bf16[1024,8960]{1,0:T(8,128)(2,1)} %get-tuple-element.37), kind=kLoop, calls=%fused_computation | loop fusion | flops 7077888 | bytes 42467328 | tf_op jit(solution)/shard_map/convert_element_type | solution.py:301
  568.1 6.6 %copy.37 = f32[1024,1536]{0,1:T(8,128)} copy(f32[1024,1536]{1,0:T(8,128)} %slice_convert_fusion.2) | data formatting | bytes 12582912 | tf_op jit(solution)/shard_map/reshape | solution.py:860
  574.6 6.6 %copy.38 = f32[1024,3,512]{2,0,1:T(8,128)} copy(f32[1024,3,512]{0,2,1:T(8,128)} %bitcast.54) | data formatting | bytes 12582912
  581.2 9.7 %copy.40 = f32[2304,1024]{1,0:T(8,128)} copy(f32[2304,1024]{0,1:T(8,128)} %get-tuple-element.62) | data formatting | bytes 18874368
  590.9 5.5 add_convert_fusion
  (110 shorter events, 56.2 us)
Async XLA Ops:
  0.6 46.7 %collective-permute-start.3 = (bf16[3,512]{1,0:T(4,128)(2,1)}, bf16[3,512]{1,0:T(4,128)(2,1)S(1)}, u32[]{:S(2)}, u32[]{:S(2)}) collective-permute-start(bf16[3,512]{1,0:T(4,128)(2,1)} %param.14), channel_id=1, source_target_pairs={{0,1},{1,0},{2,3},{3,2},{4,5},{5,4},{6,7},{7,6},{8,9},{9,8},{10,11... | collective-permute-start | bytes 9224 | tf_op jit(solution)/shard_map/ppermute | solution.py:809
  5.3 40.5 %collective-permute-start.4 = (bf16[128,1024]{1,0:T(8,128)(2,1)}, bf16[128,1024]{1,0:T(8,128)(2,1)S(1)}, u32[]{:S(2)}, u32[]{:S(2)}) collective-permute-start(bf16[128,1024]{1,0:T(8,128)(2,1)} %constant_dynamic-slice_fusion.1), channel_id=1, source_target_pairs={{0,1},{1,0},{2,3},{3,2},{4,5},{5,4},{6,7},{7,6},{8,9},{9,8},{10,11... | collective-permute-start | bytes 786440 | tf_op jit(solution)/shard_map/ppermute | solution.py:771
  5.4 142.4 %collective-permute-start.7 = (bf16[1024,1024]{1,0:T(8,128)(2,1)}, bf16[1024,1024]{1,0:T(8,128)(2,1)}, u32[]{:S(2)}, u32[]{:S(2)}) collective-permute-start(bf16[1024,1024]{1,0:T(8,128)(2,1)} %param.20), channel_id=1, source_target_pairs={{0,1},{1,0},{2,3},{3,2},{4,5},{5,4},{6,7},{7,6},{8,9},{9,8},{10,11... | collective-permute-start | bytes 6291464 | tf_op jit(solution)/shard_map/ppermute | solution.py:810
  7.3 132.7 %collective-permute-start.8 = (bf16[1024,1024]{1,0:T(8,128)(2,1)}, bf16[1024,1024]{1,0:T(8,128)(2,1)}, u32[]{:S(2)}, u32[]{:S(2)}) collective-permute-start(bf16[1024,1024]{1,0:T(8,128)(2,1)} %source.1), channel_id=1, source_target_pairs={{0,1},{1,0},{2,3},{3,2},{4,5},{5,4},{6,7},{7,6},{8,9},{9,8},{10,11... | collective-permute-start | bytes 6291464 | tf_op jit(solution)/shard_map/ppermute | solution.py:804
  12.0 8.9 %copy-start.6 = (bf16[1024,1024]{1,0:T(8,128)(2,1)S(1)}, bf16[1024,1024]{1,0:T(8,128)(2,1)}, u32[]{:S(2)}) copy-start(bf16[1024,1024]{1,0:T(8,128)(2,1)} %source.1) | copy-start | bytes 6291460
  16.8 4.6 copy-start.20
  16.8 4.6 copy-start.23
  18.9 101.2 %collective-permute-start = (bf16[256,1536]{1,0:T(8,128)(2,1)}, bf16[256,1536]{1,0:T(8,128)(2,1)}, u32[]{:S(2)}, u32[]{:S(2)}) collective-permute-start(bf16[256,1536]{1,0:T(8,128)(2,1)} %constant_dynamic-slice_fusion.2), channel_id=1, source_target_pairs={{0,1},{1,0},{2,3},{3,2},{4,5},{5,4},{6,7},{7,6},{8,9},{9,8},{10,11... | collective-permute-start | bytes 2359304 | tf_op jit(solution)/shard_map/ppermute | solution.py:771
  20.9 4.9 copy-start.22
  27.7 3.5 copy-start.16
  33.6 3.3 copy-start.19
  36.9 2.6 copy-start.21
  45.8 6.6 %collective-permute-start.5 = (bf16[128,1024]{1,0:T(8,128)(2,1)S(1)}, bf16[128,1024]{1,0:T(8,128)(2,1)S(1)}, u32[]{:S(2)}, u32[]{:S(2)}) collective-permute-start(bf16[128,1024]{1,0:T(8,128)(2,1)S(1)} %collective-permute-done.4), channel_id=1, source_target_pairs={{0,4},{2,6},{4,0},{6,2},{8,12},{10,14},{12,8},{14,10},{16,20},{18,... | collective-permute-start | bytes 786440 | tf_op jit(solution)/shard_map/ppermute | solution.py:775
  52.5 71.3 %collective-permute-start.6 = (bf16[2,128,1024]{2,1,0:T(8,128)(2,1)S(1)}, bf16[2,128,1024]{2,1,0:T(8,128)(2,1)S(1)}, u32[]{:S(2)}, u32[]{:S(2)}) collective-permute-start(bf16[2,128,1024]{2,1,0:T(8,128)(2,1)S(1)} %pad_maximum_fusion.3), channel_id=1, source_target_pairs={{0,2},{2,0},{4,6},{6,4},{8,10},{10,8},{12,14},{14,12},{16,18},{18,... | collective-permute-start | bytes 1572872 | tf_op jit(solution)/shard_map/ppermute | solution.py:777
  120.1 18.3 %collective-permute-start.1 = (bf16[256,1536]{1,0:T(8,128)(2,1)}, bf16[256,1536]{1,0:T(8,128)(2,1)S(1)}, u32[]{:S(2)}, u32[]{:S(2)}) collective-permute-start(bf16[256,1536]{1,0:T(8,128)(2,1)} %collective-permute-done), channel_id=1, source_target_pairs={{0,4},{2,6},{4,0},{6,2},{8,12},{10,14},{12,8},{14,10},{16,20},{18,... | collective-permute-start | bytes 2359304 | tf_op jit(solution)/shard_map/ppermute | solution.py:775
  123.8 16.2 %copy-start.14 = (bf16[1024,1536]{1,0:T(8,128)(2,1)S(1)}, bf16[1024,1536]{1,0:T(8,128)(2,1)}, u32[]{:S(2)}) copy-start(bf16[1024,1536]{1,0:T(8,128)(2,1)} %constant_dynamic-update-slice_fusion.3) | copy-start | bytes 9437188
  123.8 44.9 %copy-start.9 = (bf16[512,1024]{1,0:T(8,128)(2,1)}, bf16[512,1024]{1,0:T(8,128)(2,1)S(1)}, u32[]{:S(2)}) copy-start(bf16[512,1024]{1,0:T(8,128)(2,1)S(1)} %fusion.43.out_w_p) | copy-start | bytes 3145732
  138.4 3.7 copy-start.8
  139.9 13.1 %collective-permute-start.2 = (bf16[2,256,1536]{2,1,0:T(8,128)(2,1)S(1)}, bf16[2,256,1536]{2,1,0:T(8,128)(2,1)S(1)}, u32[]{:S(2)}, u32[]{:S(2)}) collective-permute-start(bf16[2,256,1536]{2,1,0:T(8,128)(2,1)S(1)} %pad_maximum_fusion.2), channel_id=1, source_target_pairs={{0,2},{2,0},{4,6},{6,4},{8,10},{10,8},{12,14},{14,12},{16,18},{18,... | collective-permute-start | bytes 4718600 | tf_op jit(solution)/shard_map/ppermute | solution.py:777
  147.7 3.2 copy-start.11
  154.5 3.4 copy-start.15
  171.8 3.2 copy-start.5
  581.2 9.7 %copy-start.1 = (bf16[1024,1024]{1,0:T(8,128)(2,1)S(1)}, bf16[1024,1024]{1,0:T(8,128)(2,1)}, u32[]{:S(2)}) copy-start(bf16[1024,1024]{1,0:T(8,128)(2,1)} %copy-done) | copy-start | bytes 6291460
  590.9 6.1 %copy-start.18 = (bf16[1024,1024]{1,0:T(8,128)(2,1)S(1)}, bf16[1024,1024]{1,0:T(8,128)(2,1)}, u32[]{:S(2)}) copy-start(bf16[1024,1024]{1,0:T(8,128)(2,1)} %get-tuple-element.96) | copy-start | bytes 6291460
  (9 other events, 13.7 us)

commit v4 on v3

--- a/solution.py
+++ b/solution.py
@@ -203,88 +203,6 @@
     return lax.dot_general(a, b, dims, preferred_element_type=F32)
 
 
-def ffn_kernel(n2, cot, wg, wu, wd, inner, gg, ug, out, n2g, acc1, acc2, *, rows):
-    step = pl.program_id(0)
-
-    @pl.when(step == 0)
-    def _():
-        acc1[...] = jnp.zeros_like(acc1)
-        acc2[...] = jnp.zeros_like(acc2)
-
-    def front(r):
-        s = pl.ds(r * rows, rows)
-        a, c = n2[s, :], cot[s, :]
-        return dot(a, wg[...]), dot(a, wu[...]), dot(c, wd[...], NT)
-
-    count = n2.shape[0] // rows
-    held = front(0)
-    for r in range(count):
-        following = front(r + 1) if r + 1 < count else None
-        s = pl.ds(r * rows, rows)
-        g, u, ig = held
-        sig = jax.nn.sigmoid(g)
-        silu = g * sig
-        low = (silu * u).astype(BF16)
-        gg_low = (ig * u * (sig + silu * (1.0 - sig))).astype(BF16)
-        ug_low = (ig * silu).astype(BF16)
-        inner[s, :] = low
-        gg[s, :] = gg_low
-        ug[s, :] = ug_low
-        acc1[s, :] += dot(low, wd[...])
-        acc2[s, :] += dot(gg_low, wg[...], NT) + dot(ug_low, wu[...], NT)
-        held = following
-
-    @pl.when(step == pl.num_programs(0) - 1)
-    def _():
-        out[...] = acc1[...].astype(out.dtype)
-        n2g[...] = acc2[...].astype(n2g.dtype)
-
-
-def ffn(n2, cot, wg, wu, wd, name):
-    rows, width = n2.shape
-    hidden = wg.shape[1]
-    tile = 256
-    full = pl.BlockSpec((rows, width), lambda h: (0, 0), pipeline_mode=pl.Buffered(1))
-
-    def col(n):
-        return pl.BlockSpec((n, tile), lambda h: (0, h))
-
-    return pl.pallas_call(
-        functools.partial(ffn_kernel, rows=256),
-        grid=(hidden // tile,),
-        in_specs=[full, full, col(width), col(width), pl.BlockSpec((tile, width), lambda h: (h, 0))],
-        out_specs=[col(rows), col(rows), col(rows), full, full],
-        out_shape=[jax.ShapeDtypeStruct((rows, hidden), BF16)] * 3
-        + [jax.ShapeDtypeStruct((rows, width), BF16)] * 2,
-        scratch_shapes=[pltpu.VMEM((rows, width), F32)] * 2,
-        name=name,
-        cost_estimate=pl.CostEstimate(
-            flops=12 * rows * width * hidden,
-            bytes_accessed=6 * hidden * width + 6 * rows * hidden + 8 * rows * width,
-            transcendentals=rows * hidden,
-        ),
-        compiler_params=pltpu.CompilerParams(vmem_limit_bytes=48 * 2**20),
-    )(n2, cot, wg, wu, wd)
-
-
-def shift_down(values, amount):
-    return jnp.pad(values, ((amount, 0), (0, 0)))[: values.shape[0]]
-
-
-def mixer_forward(normed, in_half, kernel_half):
-    channels = in_half.shape[1] // 3
-    projected = dot(normed, in_half)
-    b_part = projected[:, :channels]
-    c_part = projected[:, channels : 2 * channels]
-    x_part = projected[:, 2 * channels :]
-    mixed = b_part * x_part
-    convolved = jnp.zeros_like(mixed)
-    for k in range(KERNEL):
-        convolved = convolved + kernel_half[k] * shift_down(mixed, KERNEL - 1 - k)
-    gated = (c_part * convolved).astype(BF16)
-    return jnp.concatenate([projected.astype(BF16), convolved.astype(BF16)], axis=1), gated
-
-
 MESH = pl.DeviceIdType.MESH
 TILE = 256
 RING = 4
@@ -301,20 +219,411 @@
     return values.astype(F32)
 
 
+def inverse_rms(values):
+    return lax.rsqrt(jnp.mean(values * values, axis=-1, keepdims=True) + eps)
+
+
+STEP = 768
+PASS = 512
+
+
+def front_kernel(
+    lengths, gains, taps_own, block_input, output_grad, in_own, out_own, gate_w, up_w, down_w,
+    taps_out, cot_h, n2_h, inner_h, gg_h, ug_h, n2g_h, out_h, hidden_h, parts_o, parts_p, in_other, out_other, n1_h, gated_h,
+    in_w, out_w, src, other, n1, gated, n2, cot, wg, wu, wd, inner, gg, ug, acc1, acc2, part, hid, low1, low2, prev, taps,
+    load_sem, w_sem, o_sem, p_sem, h_sem, l_sem, x_send, x_recv, send, recv,
+):
+    rows, width = src.shape
+    channels = out_own.shape[0]
+    hidden_units = gate_w.shape[1]
+    me = lax.axis_index("dp")
+    tensor = lax.axis_index("tensor")
+    bits = [(me // (1 << k)) % 2 for k in range(3)]
+    peers = [me + (1 << k) - (2 << k) * bits[k] for k in range(3)]
+    enter([(p, tensor) for p in peers] + [(me, 1 - tensor)])
+
+    def x_copy(src_ref, dst_ref, k):
+        return pltpu.make_async_remote_copy(
+            src_ref=src_ref, dst_ref=dst_ref, send_sem=x_send.at[k], recv_sem=x_recv.at[k],
+            device_id=(me, 1 - tensor), device_id_type=MESH,
+        )
+
+    units = [(in_own.at[k], in_w.at[1, k], width) for k in range(3)] + [(out_own, out_w.at[1], channels)]
+    routes = [(1, 2, 0), (2, 1, 0), (2, 1, 0), (1, 2, 0)]
+
+    def span(u, s):
+        size = units[u][2]
+        first, second, last = routes[u]
+        if s == 0:
+            start = bits[last] * (size // 2) + bits[second] * (size // 4) + bits[first] * (size // 8)
+            return pl.ds(pl.multiple_of(start, size // 8), size // 8)
+        if s == 1:
+            start = bits[last] * (size // 2) + bits[second] * (size // 4)
+            return pl.ds(pl.multiple_of(start, size // 4), size // 4)
+        return pl.ds(pl.multiple_of(bits[last] * (size // 2), size // 2), size // 2)
+
+    def cross(u):
+        return x_copy(units[u][0].at[span(u, 0)], units[u][1].at[span(u, 0)], u)
+
+    def double(u, s):
+        at = span(u, s)
+        return pltpu.make_async_remote_copy(
+            src_ref=units[u][1].at[at], dst_ref=units[u][1].at[at],
+            send_sem=send.at[u, s], recv_sem=recv.at[u, s],
+            device_id=(peers[routes[u][s]], tensor), device_id_type=MESH,
+        )
+
+    blocks = [pl.ds(k * PASS, PASS) for k in range(rows // PASS)]
+    taps_copy = x_copy(taps_own, taps.at[1], 4)
+    input_copies = [x_copy(block_input.at[b], other.at[b], 5 + k) for k, b in enumerate(blocks)]
+    grad_copies = [
+        x_copy(output_grad.at[b], cot.at[pl.ds(rows + k * PASS, PASS)], 5 + len(blocks) + k)
+        for k, b in enumerate(blocks)
+    ]
+    taps_copy.start()
+    for u in range(4):
+        cross(u).start()
+    for copy in input_copies + grad_copies:
+        copy.start()
+
+    def load(k, src_ref, dst_ref):
+        return pltpu.make_async_copy(src_ref, dst_ref, load_sem.at[k])
+
+    first_load = load(0, block_input, src)
+    own_load = load(1, in_own, in_w.at[0])
+    out_load = load(2, out_own, out_w.at[0])
+    cot_load = load(3, output_grad, cot.at[pl.ds(0, rows)])
+    for copy in (first_load, own_load, out_load, cot_load):
+        copy.start()
+
+    steps = hidden_units // STEP
+
+    def weights(u):
+        at = pl.ds(pl.multiple_of((u % steps) * STEP, STEP), STEP)
+        slot = u % 2
+        return [
+            pltpu.make_async_copy(gate_w.at[:, at], wg.at[slot], w_sem.at[slot, 0]),
+            pltpu.make_async_copy(up_w.at[:, at], wu.at[slot], w_sem.at[slot, 1]),
+            pltpu.make_async_copy(down_w.at[at], wd.at[slot], w_sem.at[slot, 2]),
+        ]
+
+    for copy in weights(0):
+        copy.start()
+    taps[0] = taps_own[...]
+    first_load.wait()
+
+    tiles = rows // TILE
+
+    def tile_at(i, base=0):
+        return pl.ds(pl.multiple_of(base + i * TILE, TILE), TILE)
+
+    def normalize(i, carry):
+        values = widen(src[tile_at(i), :])
+        n1[tile_at(i), :] = (values * inverse_rms(values) * gains[0:1, :]).astype(BF16)
+        return carry
+
+    lax.fori_loop(0, tiles, normalize, 0)
+    n1_store = load(4, n1, n1_h)
+    n1_store.start()
+    own_load.wait()
+
+    row = lax.broadcasted_iota(jnp.int32, (TILE, channels), 0)
+
+    def mix(normed, h):
+        b_part, c_part, x_part = [dot(normed, in_w[h, k]) for k in range(3)]
+        mixed = b_part * x_part
+        last, before = prev[h, 7:8, :], prev[h, 6:7, :]
+        one = jnp.where(row == 0, last, pltpu.roll(mixed, 1, 0))
+        two = jnp.where(row == 0, before, jnp.where(row == 1, last, pltpu.roll(mixed, 2, 0)))
+        prev[h, :, :] = mixed[TILE - 8 :, :]
+        convolved = taps[h, 2:3, :] * mixed + taps[h, 1:2, :] * one + taps[h, 0:1, :] * two
+        return b_part, c_part, x_part, convolved, c_part * convolved
+
+    def part_store(h, i):
+        out = parts_o if h == 0 else parts_p
+        return pltpu.make_async_copy(part.at[i % 2], out.at[tile_at(i)], p_sem.at[i % 2])
+
+    def own_half(i, h):
+        pieces = mix(n1[tile_at(i), :], h)
+        for k in range(4):
+            part[i % 2, :, k * channels : (k + 1) * channels] = pieces[k].astype(BF16)
+        gated[tile_at(i), h * channels : (h + 1) * channels] = pieces[4].astype(BF16)
+        part_store(h, i).start()
+
+    prev[...] = jnp.zeros_like(prev)
+    for i in range(tiles):
+        if i >= 2:
+            part_store(0, i - 2).wait()
+        own_half(i, 0)
+        cross(i).wait()
+        double(i, 0).start()
+        if i >= 2:
+            double(i - 2, 0).wait()
+            double(i - 2, 1).start()
+    for u in (2, 3):
+        part_store(0, u).wait()
+        double(u, 0).wait()
+        double(u, 1).start()
+    taps_copy.wait()
+    for u in range(4):
+        double(u, 1).wait()
+        double(u, 2).start()
+
+    def masked(base, length):
+        def one(i, carry):
+            at = tile_at(i, base)
+            position = lax.broadcasted_iota(jnp.int32, (TILE, width), 0) + i * TILE
+            values = widen(cot[at, :])
+            cot[at, :] = jnp.where(position < length, values, jnp.zeros_like(values)).astype(BF16)
+            return carry
+
+        return one
+
+    own_length = jnp.where(tensor == 0, lengths[0], lengths[1])
+    other_length = jnp.where(tensor == 0, lengths[1], lengths[0])
+    cot_load.wait()
+    lax.fori_loop(0, tiles, masked(0, own_length), 0)
+    cot_store = load(5, cot.at[pl.ds(0, rows)], cot_h.at[pl.ds(0, rows)])
+    cot_store.start()
+    out_load.wait()
+    for u in range(4):
+        double(u, 2).wait()
+    other_stores = [load(6, in_w.at[1], in_other), load(7, out_w.at[1], out_other)]
+    for copy in other_stores:
+        copy.start()
+
+    def leave_mixer(values, gated_low, at):
+        hidden = values + (dot(gated_low[0], out_w[0]) + dot(gated_low[1], out_w[1]))
+        n2[at, :] = (hidden * inverse_rms(hidden) * gains[1:2, :]).astype(BF16)
+        return hidden
+
+    def hid_store(i):
+        return pltpu.make_async_copy(hid.at[i % 2], hidden_h.at[tile_at(i)], h_sem.at[i % 2])
+
+    def second_half(i, carry):
+        @pl.when(i >= 2)
+        def _():
+            part_store(1, i - 2).wait()
+            hid_store(i - 2).wait()
+
+        own_half(i, 1)
+        at = tile_at(i)
+        both = [gated[at, h * channels : (h + 1) * channels] for h in range(2)]
+        hid[i % 2] = leave_mixer(widen(src[at, :]), both, at)
+        hid_store(i).start()
+        return carry
+
+    lax.fori_loop(0, tiles, second_half, 0)
+    for i in (tiles - 2, tiles - 1):
+        part_store(1, i).wait()
+        hid_store(i).wait()
+    gated_store = load(8, gated, gated_h)
+    gated_store.start()
+    n2_store = load(9, n2.at[pl.ds(0, rows)], n2_h.at[pl.ds(0, rows)])
+    n2_store.start()
+
+    def stores(p, step, slot):
+        at = pl.ds(pl.multiple_of(p * PASS, PASS), PASS)
+        cols = pl.ds(pl.multiple_of(step * STEP, STEP), STEP)
+        return [
+            pltpu.make_async_copy(buf.at[slot], out.at[at, cols], o_sem.at[slot, k])
+            for k, (buf, out) in enumerate(((inner, inner_h), (gg, gg_h), (ug, ug_h)))
+        ]
+
+    def low_stores(p):
+        at = pl.ds(pl.multiple_of(p * PASS, PASS), PASS)
+        return [
+            pltpu.make_async_copy(low1, out_h.at[at], l_sem.at[0]),
+            pltpu.make_async_copy(low2, n2g_h.at[at], l_sem.at[1]),
+        ]
+
+    passes = 2 * rows // PASS
+
+    def ffn_pass(p, carry):
+        acc1[...] = jnp.zeros_like(acc1)
+        acc2[...] = jnp.zeros_like(acc2)
+
+        def ffn_step(step, carry):
+            u = p * steps + step
+            slot = u % 2
+            for copy in weights(u):
+                copy.wait()
+
+            @pl.when(u + 1 < passes * steps)
+            def _():
+                for copy in weights(u + 1):
+                    copy.start()
+
+            @pl.when(u >= 2)
+            def _():
+                for copy in stores(p, step, slot):
+                    copy.wait()
+
+            def front(r):
+                at = tile_at(r, p * PASS)
+                a, c = n2[at, :], cot[at, :]
+                return dot(a, wg[slot]), dot(a, wu[slot]), dot(c, wd[slot], NT)
+
+            count = PASS // TILE
+            held = front(0)
+            for r in range(count):
+                following = front(r + 1) if r + 1 < count else None
+                s = pl.ds(r * TILE, TILE)
+                g, v, ig = held
+                sig = jax.nn.sigmoid(g)
+                silu = g * sig
+                low = (silu * v).astype(BF16)
+                gg_low = (ig * v * (sig + silu * (1.0 - sig))).astype(BF16)
+                ug_low = (ig * silu).astype(BF16)
+                inner[slot, s, :] = low
+                gg[slot, s, :] = gg_low
+                ug[slot, s, :] = ug_low
+                acc1[s, :] += dot(low, wd[slot])
+                acc2[s, :] += dot(gg_low, wg[slot], NT) + dot(ug_low, wu[slot], NT)
+                held = following
+            for copy in stores(p, step, slot):
+                copy.start()
+            return carry
+
+        lax.fori_loop(0, steps, ffn_step, 0)
+
+        @pl.when(p > 0)
+        def _():
+            for copy in low_stores(p):
+                copy.wait()
+
+        low1[...] = acc1[...].astype(BF16)
+        low2[...] = acc2[...].astype(BF16)
+        for copy in low_stores(p):
+            copy.start()
+        return carry
+
+    lax.fori_loop(0, passes // 2, ffn_pass, 0)
+
+    prev[...] = jnp.zeros_like(prev)
+    for copy in input_copies:
+        copy.wait()
+
+    def other_tile(i, carry):
+        values = widen(other[tile_at(i), :])
+        normed = (values * inverse_rms(values) * gains[0:1, :]).astype(BF16)
+        both = [mix(normed, h)[4].astype(BF16) for h in range(2)]
+        leave_mixer(values, both, tile_at(i, rows))
+        return carry
+
+    lax.fori_loop(0, tiles, other_tile, 0)
+    n2_other = load(10, n2.at[pl.ds(rows, rows)], n2_h.at[pl.ds(rows, rows)])
+    n2_other.start()
+    per_block = PASS // TILE
+    for k, copy in enumerate(grad_copies):
+        copy.wait()
+        lax.fori_loop(k * per_block, (k + 1) * per_block, masked(rows, other_length), 0)
+        lax.fori_loop(passes // 2 + k, passes // 2 + k + 1, ffn_pass, 0)
+    cot_other = load(11, cot.at[pl.ds(rows, rows)], cot_h.at[pl.ds(rows, rows)])
+    cot_other.start()
+    for slot in range(2):
+        for copy in stores(0, 0, slot):
+            copy.wait()
+    for copy in low_stores(0):
+        copy.wait()
+    taps_out[...] = taps[...]
+    for copy in [n1_store, cot_store, gated_store, n2_store, n2_other, cot_other] + other_stores:
+        copy.wait()
+
+
+def front(lengths, gains, taps_own, block_input, output_grad, in_own, out_own, gate_w, up_w, down_w):
+    rows, width = block_input.shape
+    channels = out_own.shape[0]
+    hidden_units = gate_w.shape[1]
+    vmem = pl.BlockSpec(memory_space=pltpu.VMEM)
+    hbm = pl.BlockSpec(memory_space=pl.ANY)
+
+    def shaped(*shape, kind=BF16):
+        return jax.ShapeDtypeStruct(shape, kind)
+
+    both = 2 * rows
+    outs = [
+        shaped(2, KERNEL, channels, kind=F32),
+        shaped(both, width),
+        shaped(both, width),
+        shaped(both, hidden_units),
+        shaped(both, hidden_units),
+        shaped(both, hidden_units),
+        shaped(both, width),
+        shaped(both, width),
+        shaped(rows, width, kind=F32),
+        shaped(rows, 4 * channels),
+        shaped(rows, 4 * channels),
+        shaped(KERNEL, width, channels),
+        shaped(channels, width),
+        shaped(rows, width),
+        shaped(rows, 2 * channels),
+    ]
+    x_count = 5 + 2 * (rows // PASS)
+    dma = pltpu.SemaphoreType.DMA
+    return pl.pallas_call(
+        front_kernel,
+        in_specs=[pl.BlockSpec(memory_space=pltpu.SMEM), vmem, vmem] + [hbm] * 7,
+        out_specs=[vmem] + [hbm] * 14,
+        out_shape=outs,
+        scratch_shapes=[
+            pltpu.VMEM((2, KERNEL, width, channels), BF16),
+            pltpu.VMEM((2, channels, width), BF16),
+            pltpu.VMEM((rows, width), BF16),
+            pltpu.VMEM((rows, width), BF16),
+            pltpu.VMEM((rows, width), BF16),
+            pltpu.VMEM((rows, 2 * channels), BF16),
+            pltpu.VMEM((both, width), BF16),
+            pltpu.VMEM((both, width), BF16),
+            pltpu.VMEM((2, width, STEP), BF16),
+            pltpu.VMEM((2, width, STEP), BF16),
+            pltpu.VMEM((2, STEP, width), BF16),
+            pltpu.VMEM((2, PASS, STEP), BF16),
+            pltpu.VMEM((2, PASS, STEP), BF16),
+            pltpu.VMEM((2, PASS, STEP), BF16),
+            pltpu.VMEM((PASS, width), F32),
+            pltpu.VMEM((PASS, width), F32),
+            pltpu.VMEM((2, TILE, 4 * channels), BF16),
+            pltpu.VMEM((2, TILE, width), F32),
+            pltpu.VMEM((PASS, width), BF16),
+            pltpu.VMEM((PASS, width), BF16),
+            pltpu.VMEM((2, 8, channels), F32),
+            pltpu.VMEM((2, KERNEL, channels), F32),
+            dma((12,)),
+            dma((2, 3)),
+            dma((2, 3)),
+            dma((2,)),
+            dma((2,)),
+            dma((2,)),
+            dma((x_count,)),
+            dma((x_count,)),
+            dma((4, 3)),
+            dma((4, 3)),
+        ],
+        name="front",
+        cost_estimate=pl.CostEstimate(
+            flops=24 * rows * width * hidden_units, bytes_accessed=40 * hidden_units * width, transcendentals=0
+        ),
+        compiler_params=pltpu.CompilerParams(
+            collective_id=2, has_side_effects=True, vmem_limit_bytes=63 * 2**20
+        ),
+    )(lengths, gains, taps_own, block_input, output_grad, in_own, out_own, gate_w, up_w, down_w)
+
+
 def back_kernel(
     gains, taps,
-    cot_o, cot_p, n2_o, n2_p, inner_o, inner_p, gg_o, gg_p, ug_o, ug_p, n2g_o, n2g_p, out_p,
-    hidden, source, parts_o, parts_p, in_o, in_p, out_w_o, out_w_p, n1, gated_o, gated_p,
-    summed, input_grad, out_recv, small,
+    cot_h, n2_h, inner_h, gg_h, ug_h, n2g_h, out_h,
+    hidden, source, parts_o, parts_p, in_o, in_p, out_w_o, out_w_p, n1, gated,
+    summed, input_grad, block_out, out_recv, small,
     ring, rc, ry, ra, rb, rx, small_recv, cot, n2, operand, in_w, pg, part, hid, ngo, ngr, src, ig, nxt, kacc,
     load_sem, fixed_sem, tile_sem, send, recv, local_sem, x_send, x_recv, small_send, small_rsem,
 ):
     width = cot.shape[1]
-    rows = inner_o.shape[0]
-    channels = gated_o.shape[1]
-    ffn_chunks = 3 * inner_o.shape[1] // TILE
-    own_chunks = in_o.shape[1] // TILE + channels // TILE
-    in_chunks = in_o.shape[1] // TILE
+    rows = n1.shape[0]
+    channels = out_w_o.shape[0]
+    ffn_chunks = 3 * inner_h.shape[1] // TILE
+    in_chunks = 3 * channels // TILE
+    own_chunks = in_chunks + channels // TILE
     total = ffn_chunks + own_chunks
     half = width // 2
     sizes = (half, half // 2, half // 4, half // 8)
@@ -433,18 +742,14 @@
     def fixed(k, src_ref, dst_ref):
         return pltpu.make_async_copy(src_ref, dst_ref, fixed_sem.at[k])
 
-    first_loads = [fixed(0, cot_o, cot.at[pl.ds(0, rows)]), fixed(1, cot_p, cot.at[pl.ds(rows, rows)])]
-    second_loads = [fixed(2, n2_o, n2.at[pl.ds(0, rows)]), fixed(3, n2_p, n2.at[pl.ds(rows, rows)])]
-    mixer_loads = [fixed(4, in_o, in_w.at[0]), fixed(5, in_p, in_w.at[1])]
+    first_loads = [fixed(0, cot_h, cot)]
+    second_loads = [fixed(1, n2_h, n2)]
+    mixer_loads = [fixed(2, in_o, in_w.at[0]), fixed(3, in_p, in_w.at[1])]
     out_loads = [
-        fixed(6, out_w_o, cot.at[pl.ds(rows, channels)]),
-        fixed(7, out_w_p, cot.at[pl.ds(rows + channels, channels)]),
+        fixed(4, out_w_o, cot.at[pl.ds(rows, channels)]),
+        fixed(5, out_w_p, cot.at[pl.ds(rows + channels, channels)]),
     ]
-    late_loads = [fixed(8, n1, n2.at[pl.ds(0, rows)])]
-    gated_loads = [
-        fixed(9, gated_o, n2.at[pl.ds(rows, rows), pl.ds(0, channels)]),
-        fixed(10, gated_p, n2.at[pl.ds(rows, rows), pl.ds(channels, channels)]),
-    ]
+    late_loads = [fixed(6, n1, n2.at[pl.ds(0, rows)]), fixed(7, gated, n2.at[pl.ds(rows, rows)])]
 
     def start(copies):
         for copy in copies:
@@ -454,17 +759,12 @@
         for copy in copies:
             copy.wait()
 
-    groups = ((inner_o, inner_p), (gg_o, gg_p), (ug_o, ug_p))
+    groups = (inner_h, gg_h, ug_h)
     per = ffn_chunks // 3
 
     def operands(group, i, slot):
         cols = pl.ds(pl.multiple_of(i * TILE, TILE), TILE)
-        return [
-            pltpu.make_async_copy(
-                groups[group][k].at[:, cols], operand.at[slot, pl.ds(k * rows, rows)], load_sem.at[slot, k]
-            )
-            for k in range(2)
-        ]
+        return [pltpu.make_async_copy(groups[group].at[:, cols], operand.at[slot], load_sem.at[slot])]
 
     start(first_loads)
     start(operands(0, 0, 0))
@@ -474,8 +774,12 @@
     tiles = rows // TILE
 
     def n2g_block(i):
-        at = pl.ds(pl.multiple_of((tiles - 1 - i) * TILE, TILE), TILE)
-        return x_copy(n2g_p.at[at], ngr.at[at], i)
+        at = (tiles - 1 - i) * TILE
+        return x_copy(
+            n2g_h.at[pl.ds(pl.multiple_of(rows + at, TILE), TILE)],
+            ngr.at[pl.ds(pl.multiple_of(at, TILE), TILE)],
+            i,
+        )
 
     for i in range(tiles):
         n2g_block(i).start()
@@ -526,7 +830,6 @@
 
         lax.fori_loop(0, per, compute, 0)
     start(late_loads)
-    start(gated_loads)
     to_y(ffn_chunks - 1)
     done = (ffn_chunks - 1 - 8) // 2 + 1
 
@@ -540,7 +843,7 @@
         at = pl.ds(pl.multiple_of((tiles - 1 - i) * TILE, TILE), TILE)
         loads = [
             pltpu.make_async_copy(hidden.at[at], hid, tile_sem.at[0]),
-            pltpu.make_async_copy(n2g_o.at[at], ngo, tile_sem.at[1]),
+            pltpu.make_async_copy(n2g_h.at[at], ngo, tile_sem.at[1]),
             pltpu.make_async_copy(source.at[at], src, tile_sem.at[2]),
             pltpu.make_async_copy(parts_o.at[at], part.at[0], tile_sem.at[3]),
             pltpu.make_async_copy(parts_p.at[at], part.at[1], tile_sem.at[4]),
@@ -580,11 +883,10 @@
             kacc[h, 0:1, :] += jnp.sum(mixed * two, axis=0, keepdims=True)
             kacc[h, 1:2, :] += jnp.sum(mixed * one, axis=0, keepdims=True)
             kacc[h, 2:3, :] += jnp.sum(mixed * conv_grad, axis=0, keepdims=True)
-            low = jnp.concatenate(
-                [mixed_grad * x_part, gated_grad * convolved, mixed_grad * b_part], axis=1
-            ).astype(BF16)
-            pg[h, at, :] = low
-            upstream_one = upstream_one + dot(low, in_w[h], NT)
+            for k, piece_grad in enumerate((mixed_grad * x_part, gated_grad * convolved, mixed_grad * b_part)):
+                low = piece_grad.astype(BF16)
+                pg[h, at, k * channels : (k + 1) * channels] = low
+                upstream_one = upstream_one + dot(low, in_w[h, k], NT)
         values_one = widen(src[...])
         inverse_one = lax.rsqrt(jnp.mean(values_one * values_one, axis=-1, keepdims=True) + eps)
         weighted_one = upstream_one * gains[0:1, :]
@@ -602,7 +904,6 @@
     lax.fori_loop(0, tiles, mixer, 0)
     done = done + 3 * tiles
     wait(late_loads)
-    wait(gated_loads)
 
     def piece(h, m_in, m_out):
         if m_in is not None:
@@ -647,7 +948,7 @@
             scatter0(base + m).start()
             after_core(h, m - 1)
         after_core(h, own_chunks - 1)
-    last_swap = x_copy(out_p, out_recv, tiles + own_chunks)
+    last_swap = x_copy(out_h.at[pl.ds(rows, rows)], out_recv, tiles + own_chunks)
     last_swap.start()
 
     for h in range(2):
@@ -685,6 +986,25 @@
 
     lax.fori_loop(first, ffn_chunks - lead, middle, 0)
 
+    last_swap.wait()
+
+    def leave(i, carry):
+        at = pl.ds(pl.multiple_of(i * TILE, TILE), TILE)
+        loads = [
+            pltpu.make_async_copy(hidden.at[at], hid, tile_sem.at[0]),
+            pltpu.make_async_copy(out_h.at[at], ngo, tile_sem.at[1]),
+            pltpu.make_async_copy(out_recv.at[at], src, tile_sem.at[2]),
+        ]
+        start(loads)
+        wait(loads)
+        ig[...] = (hid[...] + (widen(ngo[...]) + widen(src[...]))).astype(BF16)
+        store = pltpu.make_async_copy(ig, block_out.at[at], tile_sem.at[5])
+        store.start()
+        store.wait()
+        return carry
+
+    lax.fori_loop(0, tiles, leave, 0)
+
     def drain(k, carry):
         tick(k)
         finish(k - lead)
@@ -693,7 +1013,6 @@
     lax.fori_loop(ffn_chunks, total + 4, drain, 0)
     lax.fori_loop(total + 4 - lead, total, middle, 0)
     gather(0, total - 1).wait()
-    last_swap.wait()
 
 
 def back(gains, taps, arrays, rows, width, hidden, channels):
@@ -710,9 +1029,10 @@
     return pl.pallas_call(
         back_kernel,
         in_specs=[vmem, vmem] + [hbm] * len(arrays),
-        out_specs=[hbm, hbm, hbm, vmem],
+        out_specs=[hbm, hbm, hbm, hbm, vmem],
         out_shape=[
             jax.ShapeDtypeStruct((width, total * TILE), BF16),
+            jax.ShapeDtypeStruct((rows, width), BF16),
             jax.ShapeDtypeStruct((rows, width), BF16),
             jax.ShapeDtypeStruct((rows, width), BF16),
             jax.ShapeDtypeStruct((8, width), F32),
@@ -728,7 +1048,7 @@
             pltpu.VMEM((2 * rows, width), BF16),
             pltpu.VMEM((2 * rows, width), BF16),
             buffer(2, 2 * rows),
-            pltpu.VMEM((2, width, 3 * channels), BF16),
+            pltpu.VMEM((2, 3, width, channels), BF16),
             pltpu.VMEM((2, rows, 3 * channels), BF16),
             pltpu.VMEM((2, TILE, 4 * channels), BF16),
             pltpu.VMEM((TILE, width), F32),
@@ -738,8 +1058,8 @@
             pltpu.VMEM((TILE, width), BF16),
             pltpu.VMEM((2, 8, channels), F32),
             pltpu.VMEM((2, 8, channels), F32),
-            pltpu.SemaphoreType.DMA((2, 2)),
-            pltpu.SemaphoreType.DMA((11,)),
+            pltpu.SemaphoreType.DMA((2,)),
+            pltpu.SemaphoreType.DMA((8,)),
             pltpu.SemaphoreType.DMA((6,)),
             pltpu.SemaphoreType.DMA((8, total + own_chunks)),
             pltpu.SemaphoreType.DMA((8, total + own_chunks)),
@@ -765,20 +1085,64 @@
     return j < 0
 
 
-def quarter_gather(weight, rows_axis_quarter, dp_index):
-    rows = weight.shape[0] // 4
-    sliced = lax.dynamic_slice_in_dim(weight, rows_axis_quarter * rows, rows, axis=0)
-    first = lax.ppermute(sliced, "tensor", [(0, 1), (1, 0)])
-    n_dp = lax.axis_size("dp")
-    flip_y = [(i, i ^ 2) for i in range(n_dp)]
-    flip_c = [(i, i ^ 1) for i in range(n_dp)]
-    from_y = lax.ppermute(first, "dp", flip_y)
-    both = jnp.stack([first, from_y])
-    from_c = lax.ppermute(both, "dp", flip_c)
-    out = weight
-    for piece, which in ((both[0], 0), (both[1], 2), (from_c[0], 1), (from_c[1], 3)):
-        out = lax.dynamic_update_slice_in_dim(out, piece, (rows_axis_quarter ^ which) * rows, axis=0)
-    return out
+def finish_kernel(summed, down, gate, up, in_grad, out, *, per, in_count):
+    j = pl.program_id(0)
+    values = widen(summed[...])
+
+    @pl.when(j < per)
+    def _():
+        down[...] = values.T
+
+    @pl.when((j >= per) & (j < 2 * per))
+    def _():
+        gate[...] = values
+
+    @pl.when((j >= 2 * per) & (j < 3 * per))
+    def _():
+        up[...] = values
+
+    @pl.when((j >= 3 * per) & (j < 3 * per + in_count))
+    def _():
+        in_grad[0] = values
+
+    @pl.when(j >= 3 * per + in_count)
+    def _():
+        out[...] = values.T
+
+
+def finish_grads(summed, hidden_units, channels):
+    width, columns = summed.shape
+    per, halves = hidden_units // TILE, channels // TILE
+    in_count = KERNEL * halves
+
+    def clamp(j, low, count):
+        return jnp.minimum(jnp.maximum(j - low, 0), count - 1)
+
+    def in_map(j):
+        m = clamp(j, 3 * per, in_count)
+        return (m // halves, 0, m % halves)
+
+    return pl.pallas_call(
+        functools.partial(finish_kernel, per=per, in_count=in_count),
+        grid=(columns // TILE,),
+        in_specs=[pl.BlockSpec((width, TILE), lambda j: (0, j))],
+        out_specs=[
+            pl.BlockSpec((TILE, width), lambda j: (clamp(j, 0, per), 0)),
+            pl.BlockSpec((width, TILE), lambda j: (0, clamp(j, per, per))),
+            pl.BlockSpec((width, TILE), lambda j: (0, clamp(j, 2 * per, per))),
+            pl.BlockSpec((1, width, TILE), in_map),
+            pl.BlockSpec((TILE, width), lambda j: (clamp(j, 3 * per + in_count, halves), 0)),
+        ],
+        out_shape=[
+            jax.ShapeDtypeStruct((hidden_units, width), F32),
+            jax.ShapeDtypeStruct((width, hidden_units), F32),
+            jax.ShapeDtypeStruct((width, hidden_units), F32),
+            jax.ShapeDtypeStruct((KERNEL, width, channels), F32),
+            jax.ShapeDtypeStruct((channels, width), F32),
+        ],
+        name="finish_grads",
+        compiler_params=pltpu.CompilerParams(vmem_limit_bytes=48 * 2**20),
+    )(summed)
 
 
 def fast(
@@ -794,82 +1158,46 @@
     output_grad,
     lengths,
 ):
-    rows = block_input.shape[0]
-    channels = in_weight.shape[2]
+    rows, width = block_input.shape
+    channels, hidden_units = out_weight.shape[0], gate_weight.shape[1]
     me = lax.axis_index("tensor")
-    dp_index = lax.axis_index("dp")
-    swap = [(0, 1), (1, 0)]
-    quarter = dp_index % 4
-
-    other_input = lax.ppermute(block_input, "tensor", swap)
-    in_shape = in_weight.shape
-    in_weight = in_weight.reshape(in_shape[0], 3 * channels)
-    in_other = quarter_gather(in_weight, quarter, dp_index)
-    out_other = quarter_gather(out_weight, quarter, dp_index)
-    kernel_other = lax.ppermute(conv_kernel, "tensor", swap).astype(F32)
-    other_grad = lax.ppermute(output_grad, "tensor", swap)
-    kernel_own = conv_kernel.astype(F32)
-
-    position = jnp.arange(rows, dtype=jnp.int32)
-    mask_own = (position < lengths[me])[:, None]
-    mask_other = (position < lengths[1 - me])[:, None]
-    cot_own = jnp.where(mask_own, output_grad, jnp.zeros_like(output_grad))
-    cot_other = jnp.where(mask_other, other_grad, jnp.zeros_like(other_grad))
-
-    def forward(source_low):
-        source = source_low.astype(F32)
-        normed = rms_forward(source, mixer_gain)[0]
-        normed = normed.astype(BF16)
-        parts = [
-            mixer_forward(normed, w, k)
-            for w, k in ((in_weight, kernel_own), (in_other, kernel_other))
-        ]
-        hidden = source + (dot(parts[0][1], out_weight) + dot(parts[1][1], out_other))
-        normed_two = rms_forward(hidden, ffn_gain)[0]
-        return normed, parts, hidden, normed_two.astype(BF16)
-
-    normed_one, parts, hidden, n2_own = forward(block_input)
-    n2_other = forward(other_input)[3]
-
-    inner_o, gg_o, ug_o, out_o, n2g_o = ffn(n2_own, cot_own, gate_weight, up_weight, down_weight, "ffn_own")
-    inner_p, gg_p, ug_p, out_p, n2g_p = ffn(
-        n2_other, cot_other, gate_weight, up_weight, down_weight, "ffn_other"
-    )
-    width, hidden_units = gate_weight.shape
-    summed, input_grad, out_recv, small = back(
-        jnp.stack([mixer_gain, ffn_gain]),
-        jnp.stack([kernel_own, kernel_other]),
-        (
-            cot_own, cot_other, n2_own, n2_other, inner_o, inner_p, gg_o, gg_p, ug_o, ug_p, n2g_o, n2g_p, out_p,
-            hidden, block_input, parts[0][0], parts[1][0], in_weight, in_other, out_weight, out_other,
-            normed_one, parts[0][1], parts[1][1],
-        ),
-        rows,
-        width,
-        hidden_units,
-        channels,
-    )
-    block_output = (hidden + (widen(out_o) + widen(out_recv))).astype(BF16)
+    gains = jnp.stack([mixer_gain, ffn_gain])
+    in_parts = jnp.transpose(in_weight, (1, 0, 2))
+    taps, cot, n2, inner, gg, ug, n2g, out, hidden, parts_o, parts_p, in_other, out_other, n1, gated = front(
+        lengths,
+        gains,
+        conv_kernel.astype(F32),
+        block_input,
+        output_grad,
+        in_parts,
+        out_weight,
+        gate_weight,
+        up_weight,
+        down_weight,
+    )
+    arrays = (cot, n2, inner, gg, ug, n2g, out, hidden, block_input, parts_o, parts_p)
+    arrays += (in_parts, in_other, out_weight, out_other, n1, gated)
+    summed, input_grad, block_output, _, small = back(gains, taps, arrays, rows, width, hidden_units, channels)
+    down_grad, gate_grad, up_grad, in_grad, out_grad = finish_grads(summed, hidden_units, channels)
     conv_kernel_grad = lax.dynamic_slice_in_dim(small[2 : 2 + KERNEL], me * channels, channels, axis=1)
-    splits = [hidden_units, 2 * hidden_units, 3 * hidden_units, 3 * hidden_units + 3 * channels]
-    down_grad, gate_grad, up_grad, in_grad, out_grad = jnp.split(summed, splits, axis=1)
     return (
         block_output,
         input_grad,
         small[0],
-        widen(in_grad).reshape(in_shape),
+        jnp.transpose(in_grad, (1, 0, 2)),
         conv_kernel_grad,
-        widen(out_grad.T),
+        out_grad,
         small[1],
-        widen(gate_grad),
-        widen(up_grad),
-        widen(down_grad.T),
+        gate_grad,
+        up_grad,
+        down_grad,
     )
 
 
 def solution(mesh):
     def step(*args):
-        one_slot_each = mesh.shape["tensor"] == 2 and args[10].shape[0] == 2 and mesh.shape["dp"] == 16
+        rows, slots = args[0].shape[0], args[10].shape[0]
+        one_slot_each = mesh.shape["tensor"] == 2 and mesh.shape["dp"] == 16 and slots == 2 and rows == 4 * TILE
         return (fast if one_slot_each else local)(*args)
 
     return jax.shard_map(

time: 609 us -> 474 us (0.78)
  Pallas kernels: 361 us -> 456 us
  waiting for transfers between devices: 86.6 us -> 0 us
  local copies, waits for them, and re-layouts: 60.6 us -> 5.62 us
  other arithmetic: 51.6 us -> 2.6 us
  matrix products: 27.2 us -> 0 us
  starting transfers between devices: 10.2 us -> 0 us
    ppermute x9 -> x0, waiting for transfers between devices: 86.6 us -> none  [the longest x2 66.9 us: quarter_gather(): first = lax.ppermute(sliced, 'tensor', [(0, 1), (1, 0)])]
    pallas_call x2, Pallas kernels: 75.2 us -> 159 us  [the longest x1 128 us: front(): pl.pallas_call(front_kernel, in_specs=[pl.BlockSpec(memory_space=pltpu.SM...]
    unnamed x55 -> x6, local copies, waits for them, and re-layouts: 39.7 us -> 4.41 us
    dot_general x8 -> x0, matrix products: 27.2 us -> none  [dot(): return lax.dot_general(a, b, dims, preferred_element_type=F32)]
    convert_element_type x9 -> x1, other arithmetic: 25.7 us -> 1.29 us  [fast(): conv_kernel.astype(F32)]
    reshape x2 -> x0, local copies, waits for them, and re-layouts: 11.4 us -> none  [the longest x1 6.56 us: fast(): widen(in_grad).reshape(in_shape)]
    pallas_call x1, Pallas kernels: 286 us -> 297 us  [back(): pl.pallas_call(back_kernel, in_specs=[vmem, vmem] + [hbm] * len(arrays),...]
    ppermute x9 -> x0, starting transfers between devices: 10.2 us -> none  [the longest x2 3.03 us: quarter_gather(): from_y = lax.ppermute(first, 'dp', flip_y)]
  transfers between devices with their start and end apart: 9 -> 0, of which waited for: 3 -> 0; matrix products, arithmetic and copies ran while one was open for 9% -> 0% of each run, Pallas kernels for 0% -> 0%
where the time goes in v4:
time: 474 us; the launch traced here: 466 us
  Pallas kernels  456 us (96%)
  local copies, waits for them, and re-layouts  5.62 us (1%)
    pallas_call x1, Pallas kernels, back(): pl.pallas_call(back_kernel, in_specs=[vmem, vmem] + [hbm] * len(arrays),...  297 us
    pallas_call x1, Pallas kernels, front(): pl.pallas_call(front_kernel, in_specs=[pl.BlockSpec(memory_space=pltpu.SM...  128 us
    pallas_call x1, Pallas kernels, finish_grads(): pl.pallas_call(functools.partial(finish_kernel, per=per, in_count=in_coun...  31.5 us

profile of v4, /device:TPU:0, one launch (start us, length us, event | category | flops | bytes accessed | tf_op | source)
XLA Modules:
  0.0 465.7 jit_solution(6869127762955748393)
XLA Ops:
  0.6 1.3 pad_maximum_fusion.gains
  2.0 1.3 convert_element_type.3.taps_own
  3.2 127.9 %front.1 = (f32[2,3,512]{2,1,0:T(4,128)}, bf16[2048,1024]{1,0:T(8,128)(2,1)}, bf16[2048,1024]{1,0:T(8,128)(2,1)}, bf16[2048,2304]{1,0:T(8,128)(2,1)}, bf16[2048,...) custom-call(s32[2]{0:T(128)} %lengths.1, ...), custom_call_target="tpu_custom_call" | custom-call | flops 57982058496 | bytes 94371840 | tf_op jit(solution)/shard_map/front/pallas_call | solution.py:564
  131.1 296.9 %back.1 = (bf16[1024,8960]{1,0:T(8,128)(2,1)}, bf16[1024,1024]{1,0:T(8,128)(2,1)}, bf16[1024,1024]{1,0:T(8,128)(2,1)}, bf16[1024,1024]{1,0:T(8,128)(2,1)}, f32[8,1024]{1,0:T(8,128)}) custom-call(f32[2,1024]{1,0:T(2,128)} %pad_maximum_fusion.gains, f32[2,3,512]{2,1,0:T(4,128)} %get-tuple-element.34.taps, bf16[2048,1024]{1,0:T(8,128)(2,1)} %get-tuple-element.35.cot_h, ...), custom_call_target="tpu_custom_call" | custom-call | flops 46170898432 | bytes 47185920 | tf_op jit(solution)/shard_map/back/pallas_call | solution.py:1029
  428.0 0.0 copy-start.1
  428.0 31.5 %finish_grads.1 = (f32[2304,1024]{1,0:T(8,128)}, f32[1024,2304]{1,0:T(8,128)}, f32[1024,2304]{1,0:T(8,128)}, f32[3,1024,512]{2,1,0:T(8,128)}, f32[512,1024]{1,0:T(8,128)}) custom-call(bf16[1024,8960]{1,0:T(8,128)(2,1)} %get-tuple-element.52.summed), custom_call_target="tpu_custom_call" | custom-call | tf_op jit(solution)/shard_map/finish_grads/pallas_call | solution.py:1125
  459.6 0.0 copy-start
  459.6 0.0 copy-done.1
  459.6 0.6 constant_dynamic-slice_fusion
  460.2 0.6 fusion
  460.8 3.1 copy.23
  463.9 0.0 copy-done
  463.9 1.3 copy.24
  (1 shorter events, 0.0 us)
Async XLA Ops:
  428.0 31.6 %copy-start.1 = (f32[8,1024]{1,0:T(8,128)S(1)}, f32[8,1024]{1,0:T(8,128)}, u32[]{:S(2)}) copy-start(f32[8,1024]{1,0:T(8,128)} %get-tuple-element.51) | copy-start | bytes 98308
  459.6 4.3 copy-start
